TPU v7x, 512 devices: a whole 4x4x16 slice. The times are simulated.
512 devices in a mesh: gx: 128 (over y, x_hi, z), gz: 4 (over x_lo, core).
Axes of the slice: x: 4 (x_hi: 2, x_lo: 2; x = x_hi * 2 + x_lo), y: 4, z: 16, core: 2. Of those that a mesh axis runs over, the one named last changes fastest.
Arguments:
- pressure: float32 [64, 2048, 256], P('gz', 'gx'), may hold values from -6 to 6
- saturation: float32 [64, 2048, 256], P('gz', 'gx'), may hold values from 0.05 to 0.8
- sat_history: float32 [64, 2048, 256], P('gz', 'gx'), may hold values from 0.05 to 0.85, as said below
- storage: float32 [64, 2048, 256], P('gz', 'gx'), may hold values from 0.3 to 3
- step_volume: float32 [64, 2048, 256], P('gz', 'gx'), may hold values from 0.005 to 0.05
- transmiss: float32 [3, 64, 2048, 256], P(None, 'gz', 'gx'), may hold values from 0.1 to 2
- perf_cell: int32 [4096, 16], P('gx'), may hold values from 0 to 262143, as said below
- perf_index: float32 [4096, 16], P('gx'), may hold values from 0.2 to 2
- control: int32 [4096], P('gx'), may hold values from 0 to 1
- target: float32 [4096], P('gx'), may hold values from 0.5 to 3
Outputs:
- new_pressure: float32 [64, 2048, 256], P('gz', 'gx')
- residual: float32 [64, 2048, 256], P('gz', 'gx')
- new_saturation: float32 [64, 2048, 256], P('gz', 'gx')
- new_history: float32 [64, 2048, 256], P('gz', 'gx')
- bottom_hole: float32 [4096], P('gx')
Inputs may be any that keep to these rules, and one draw needn't show every extreme that they name: `perf_cell`: each perforation number names a cell of its own well's row of tiles, counted as layer * 16 * 256 + first lateral index within the row * 256 + second lateral index; a well's perforations lie in 16 consecutive layers, one a layer, top first, and from one to the next each lateral index moves by at most one cell. sat_history is at least the cell's saturation.
All inputs are finite; a program needn't handle non-finite values.
Results may differ from a plain program's by a relative error of at most 0.0003.
Values sent between devices are 32-bit elements; how exact they have to be, the bound alone decides.
A program may use at most 64 MiB of HBM per device.

v0:
```python
import jax
import jax.numpy as jnp
from jax import lax
from jax.sharding import PartitionSpec as P

SWEEPS = 4


def padded(block, sides, width):
    for axis, dim in sides:
        count = lax.axis_size(axis)
        forward = [(i, i + 1) for i in range(count - 1)]
        backward = [(target, source) for source, target in forward]
        low = lax.ppermute(
            lax.slice_in_dim(block, block.shape[dim] - width, None, axis=dim), axis, forward
        )
        high = lax.ppermute(lax.slice_in_dim(block, 0, width, axis=dim), axis, backward)
        block = jnp.concatenate([low, block, high], axis=dim)
    return block


def mobility(sat, history):
    trapped = history / (1.0 + 1.5 * history)
    excess = jnp.maximum(sat - trapped, 0.0)
    free_gas = 0.5 * (excess + jnp.sqrt(excess * excess + excess / 0.375))
    relperm = jnp.where(sat < history, free_gas * free_gas, sat * sat)
    gas = relperm / 0.5
    total = (1.0 - sat) * (1.0 - sat) + gas
    return (total, gas / total)


def column_next(field):
    return jnp.concatenate([field[..., 1:], jnp.zeros_like(field[..., :1])], axis=-1)


def column_prev(field):
    return jnp.concatenate([jnp.zeros_like(field[..., :1]), field[..., :-1]], axis=-1)


def beside(extended):
    center = extended[1:-1, 1:-1]
    pairs = (
        (extended[2:, 1:-1], extended[:-2, 1:-1]),
        (extended[1:-1, 2:], extended[1:-1, :-2]),
        (column_next(center), column_prev(center)),
    )
    return (center, pairs)


def pressure_halo(field):
    return padded(field, (("gx", 1), ("gz", 0)), 1)


def operate(extended, storage, terms):
    center, pairs = beside(extended)
    result = storage * center
    for (plus, minus), (upper, lower) in zip(terms, pairs):
        result = result + plus * (center - upper) + minus * (center - lower)
    return result


def body(
    pressure,
    saturation,
    sat_history,
    storage,
    step_volume,
    transmiss,
    perf_cell,
    perf_index,
    control,
    target,
):
    layers, rows, columns = pressure.shape
    total, frac = mobility(saturation, sat_history)
    stacked = jnp.stack([total, frac, transmiss[0], transmiss[1]])
    widened = padded(stacked, (("gx", 2), ("gz", 1)), 1)
    total_ext, frac_ext = (widened[0], widened[1])
    layer_minus = widened[2][0:layers, 1 : rows + 1]
    row_minus = widened[3][1 : layers + 1, 0:rows]
    layer_global = lax.axis_index("gz") * layers + lax.broadcasted_iota(
        jnp.int32, pressure.shape, 0
    )
    row_global = lax.axis_index("gx") * rows + lax.broadcasted_iota(jnp.int32, pressure.shape, 1)
    column_local = lax.broadcasted_iota(jnp.int32, pressure.shape, 2)
    plus_faces = (
        jnp.where(layer_global < layers * lax.axis_size("gz") - 1, transmiss[0], 0.0),
        jnp.where(row_global < rows * lax.axis_size("gx") - 1, transmiss[1], 0.0),
        jnp.where(column_local < columns - 1, transmiss[2], 0.0),
    )
    minus_faces = (layer_minus, row_minus, column_prev(transmiss[2]))
    center_total, total_pairs = beside(total_ext)
    terms = []
    diag = storage
    for plus_t, minus_t, (upper, lower) in zip(plus_faces, minus_faces, total_pairs):
        plus = plus_t * 0.5 * (center_total + upper)
        minus = minus_t * 0.5 * (center_total + lower)
        terms.append((plus, minus))
        diag = diag + plus + minus
    cells = layers * rows * columns
    local_index = perf_cell - lax.axis_index("gz") * cells
    inside = (local_index >= 0) & (local_index < cells)
    safe_index = jnp.clip(local_index, 0, cells - 1)
    flat_pressure = pressure.reshape(-1)
    cell_p = flat_pressure[safe_index]
    weight = jnp.where(inside, perf_index * total.reshape(-1)[safe_index], 0.0)
    part_p = jnp.sum(weight * cell_p, axis=1)
    part_w = jnp.sum(weight, axis=1)
    sum_p, sum_w = lax.psum((part_p, part_w), "gz")
    bottom_hole = jnp.where(control == 0, (target + sum_p) / sum_w, target)
    rate = weight * (bottom_hole[:, None] - cell_p)
    source = (
        jnp.zeros((cells,), jnp.float32)
        .at[safe_index.reshape(-1)]
        .add(rate.reshape(-1))
        .reshape(pressure.shape)
    )
    rhs = storage * pressure + source
    field = pressure
    for sweep in range(SWEEPS):
        field = field + (rhs - operate(pressure_halo(field), storage, terms)) / diag
    field_ext = pressure_halo(field)
    residual = rhs - operate(field_ext, storage, terms)
    center_frac, frac_pairs = beside(frac_ext)
    center_p, field_pairs = beside(field_ext)
    out = jnp.zeros_like(field)
    for (plus, minus), (upper_p, lower_p), (upper_f, lower_f) in zip(
        terms, field_pairs, frac_pairs
    ):
        flow_up = plus * (center_p - upper_p)
        out = out + flow_up * jnp.where(flow_up > 0, center_frac, upper_f)
        flow_down = minus * (center_p - lower_p)
        out = out + flow_down * jnp.where(flow_down > 0, center_frac, lower_f)
    gas_source = jnp.maximum(source, 0.0) + jnp.minimum(source, 0.0) * frac
    new_saturation = saturation + step_volume * (gas_source - out)
    new_history = jnp.maximum(sat_history, new_saturation)
    return (field, residual, new_saturation, new_history, bottom_hole)


def solution(mesh):
    return jax.shard_map(
        body,
        mesh=mesh,
        in_specs=(
            P("gz", "gx", None),
            P("gz", "gx", None),
            P("gz", "gx", None),
            P("gz", "gx", None),
            P("gz", "gx", None),
            P(None, "gz", "gx", None),
            P("gx", None),
            P("gx", None),
            P("gx"),
            P("gx"),
        ),
        out_specs=(
            P("gz", "gx", None),
            P("gz", "gx", None),
            P("gz", "gx", None),
            P("gz", "gx", None),
            P("gx"),
        ),
        check_vma=False,
    )
```

profile of v0, /device:TPU:26, one launch (start us, length us, event | category | flops | bytes accessed | tf_op | source)
XLA Modules:
  0.0 143.2 jit_solution(14789003180040027547)
XLA Ops:
  0.6 1.1 slice.271
  1.8 1.3 fusion.102
  3.1 0.7 pad_maximum_fusion.48
  3.9 3.8 %collective-permute-start = (f32[4,16,1,256]{3,2,1,0:T(1,128)}, f32[4,16,1,256]{3,2,1,0:T(1,128)S(1)}, u32[]{:S(2)}, u32[]{:S(2)}) collective-permute-start(f32[4,16,1,256]{3,2,1,0:T(1,128)} %get-tuple-element.27), channel_id=1, source_target_pairs={{0,4},{4,8},{8,12},{12,16},{16,20},{20,24},{24,28},{28,32},{32,36}... | collective-permute-start | bytes 196616 | tf_op jit(solution)/shard_map/ppermute | solution.py:14
  7.7 11.2 %collective-permute-start.1 = (f32[4,16,1,256]{3,2,1,0:T(1,128)}, f32[4,16,1,256]{3,2,1,0:T(1,128)S(1)}, u32[]{:S(2)}, u32[]{:S(2)}) collective-permute-start(f32[4,16,1,256]{3,2,1,0:T(1,128)} %get-tuple-element.28), channel_id=1, source_target_pairs={{4,0},{8,4},{12,8},{16,12},{20,16},{24,20},{28,24},{32,28},{36,32}... | collective-permute-start | bytes 196616 | tf_op jit(solution)/shard_map/ppermute | solution.py:17
  19.0 0.6 fusion.120
  19.6 1.9 %collective-permute-start.4 = (f32[16,1,256]{2,1,0:T(1,128)}, f32[16,1,256]{2,1,0:T(1,128)}, u32[]{:S(2)}, u32[]{:S(2)}) collective-permute-start(f32[16,1,256]{2,1,0:T(1,128)} %get-tuple-element.65), channel_id=1, source_target_pairs={{0,4},{4,8},{8,12},{12,16},{16,20},{20,24},{24,28},{28,32},{32,36}... | collective-permute-start | bytes 49160 | tf_op jit(solution)/shard_map/ppermute | solution.py:14
  21.5 8.4 %collective-permute-start.5 = (f32[16,1,256]{2,1,0:T(1,128)}, f32[16,1,256]{2,1,0:T(1,128)}, u32[]{:S(2)}, u32[]{:S(2)}) collective-permute-start(f32[16,1,256]{2,1,0:T(1,128)} %get-tuple-element.64), channel_id=1, source_target_pairs={{4,0},{8,4},{12,8},{16,12},{20,16},{24,20},{28,24},{32,28},{36,32}... | collective-permute-start | bytes 49160 | tf_op jit(solution)/shard_map/ppermute | solution.py:17
  30.0 0.1 fusion.119
  30.2 0.6 compare_select_fusion
  30.8 0.1 reshape.61
  30.9 0.1 copy.17
  31.1 3.1 %gather_fusion = f32[512]{0:T(512)S(1)} fusion(f32[65536]{0:T(1024)S(1)} %bitcast.37, s32[1024]{0:T(1024)S(1)} %pad_clamp_fusion), kind=kCustom, calls=%fused_computation | custom fusion | bytes 6144 | tf_op jit(solution)/shard_map/gather | solution.py:106
  34.3 0.1 copy.18
  34.5 3.1 %gather_fusion.1 = f32[512]{0:T(512)S(1)} fusion(f32[65536]{0:T(1024)S(1)} %bitcast.38, s32[1024]{0:T(1024)S(1)} %pad_clamp_fusion), kind=kCustom, calls=%fused_computation.1 | custom fusion | bytes 6144 | tf_op jit(solution)/shard_map/gather | solution.py:105
  37.8 0.1 multiply_reduce_fusion
  37.9 5.7 %all-reduce.15 = (f32[32]{0:T(128)S(1)}, f32[32]{0:T(128)S(1)}) all-reduce(f32[32]{0:T(128)S(1)} %get-tuple-element.6, f32[32]{0:T(128)S(1)} %get-tuple-element.5), channel_id=1, replica_groups=mesh['gx'=128,'gz'=4] {'gz'}, use_global_device_ids=true, to_apply=%region_3.4 | all-reduce | flops 64 | bytes 512 | tf_op jit(solution)/shard_map/psum | solution.py:109
  43.7 0.1 reshape.79
  43.8 0.1 reshape.54
  43.9 3.7 %scatter_custom_fusion = f32[65536]{0:T(1024)S(1)} fusion(s32[512]{0:T(512)S(1)} %bitcast.42, f32[512]{0:T(512)S(1)} %reshape.79, f32[]{:T(128)} %constant.16.clone.1), kind=kCustom, calls=%fused_computation.169 | custom fusion | flops 512 | bytes 262148 | tf_op jit(solution)/shard_map/scatter-add | solution.py:115
  47.8 2.0 %collective-permute-start.2 = (f32[4,1,18,256]{3,2,1,0:T(8,128)S(1)}, f32[4,1,18,256]{3,2,1,0:T(8,128)S(1)}, u32[]{:S(2)}, u32[]{:S(2)}) collective-permute-start(f32[4,1,18,256]{3,2,1,0:T(8,128)S(1)} %get-tuple-element.25), channel_id=1, source_target_pairs={{0,1},{1,2},{2,3},{4,5},{5,6},{6,7},{8,9},{9,10},{10,11},{12,13},{... | collective-permute-start | bytes 221192 | tf_op jit(solution)/shard_map/ppermute | solution.py:14
  49.8 3.5 %collective-permute-start.3 = (f32[4,1,18,256]{3,2,1,0:T(8,128)S(1)}, f32[4,1,18,256]{3,2,1,0:T(8,128)S(1)}, u32[]{:S(2)}, u32[]{:S(2)}) collective-permute-start(f32[4,1,18,256]{3,2,1,0:T(8,128)S(1)} %get-tuple-element.26), channel_id=1, source_target_pairs={{1,0},{2,1},{3,2},{5,4},{6,5},{7,6},{9,8},{10,9},{11,10},{13,12},{... | collective-permute-start | bytes 221192 | tf_op jit(solution)/shard_map/ppermute | solution.py:17
  53.4 0.7 pad_maximum_fusion.63
  54.1 1.9 %collective-permute-start.6 = (f32[1,18,256]{2,1,0:T(8,128)S(1)}, f32[1,18,256]{2,1,0:T(8,128)S(1)}, u32[]{:S(2)}, u32[]{:S(2)}) collective-permute-start(f32[1,18,256]{2,1,0:T(8,128)S(1)} %get-tuple-element.44), channel_id=1, source_target_pairs={{1,0},{2,1},{3,2},{5,4},{6,5},{7,6},{9,8},{10,9},{11,10},{13,12},{... | collective-permute-start | bytes 55304 | tf_op jit(solution)/shard_map/ppermute | solution.py:17
  56.0 2.4 %collective-permute-start.7 = (f32[1,18,256]{2,1,0:T(8,128)S(1)}, f32[1,18,256]{2,1,0:T(8,128)S(1)}, u32[]{:S(2)}, u32[]{:S(2)}) collective-permute-start(f32[1,18,256]{2,1,0:T(8,128)S(1)} %get-tuple-element.45), channel_id=1, source_target_pairs={{0,1},{1,2},{2,3},{4,5},{5,6},{6,7},{8,9},{9,10},{10,11},{12,13},{... | collective-permute-start | bytes 55304 | tf_op jit(solution)/shard_map/ppermute | solution.py:14
  58.4 0.3 pad_maximum_fusion
  58.7 0.1 slice_bitcast_fusion
  58.9 0.1 fusion.110
  59.0 2.1 %collective-permute-done.7 = f32[1,18,256]{2,1,0:T(8,128)S(1)} collective-permute-done((f32[1,18,256]{2,1,0:T(8,128)S(1)}, f32[1,18,256]{2,1,0:T(8,128)S(1)}, u32[]{:S(2)}, u32[]{:S(2)}) %collective-permute-start.7) | collective-permute-done | bytes 18464 | tf_op jit(solution)/shard_map/ppermute | solution.py:14
  61.2 1.5 %fusion.84 = (f32[16,16,256]{2,1,0:T(8,128)S(1)}, f32[16,16,256]{2,1,0:T(8,128)S(1)}, f32[16,16,256]{2,1,0:T(8,128)S(1)}, f32[16,16,256]{2,1,0:T(8,128)S(1)}, f3...) fusion(f32[16,16,256]{2,1,0:T(8,128)S(1)} %copy-done, ...), kind=kLoop, calls=%fused_computation.130 | loop fusion | flops 3801088 | bytes 6618400 | tf_op jit(solution)/shard_map/add | solution.py:121
  62.7 1.9 %collective-permute-start.8 = (f32[16,1,256]{2,1,0:T(1,128)S(1)}, f32[16,1,256]{2,1,0:T(1,128)S(1)}, u32[]{:S(2)}, u32[]{:S(2)}) collective-permute-start(f32[16,1,256]{2,1,0:T(1,128)S(1)} %get-tuple-element.61), channel_id=1, source_target_pairs={{0,4},{4,8},{8,12},{12,16},{16,20},{20,24},{24,28},{28,32},{32,36}... | collective-permute-start | bytes 49160 | tf_op jit(solution)/shard_map/ppermute | solution.py:14
  64.7 8.4 %collective-permute-start.9 = (f32[16,1,256]{2,1,0:T(1,128)S(1)}, f32[16,1,256]{2,1,0:T(1,128)S(1)}, u32[]{:S(2)}, u32[]{:S(2)}) collective-permute-start(f32[16,1,256]{2,1,0:T(1,128)S(1)} %get-tuple-element.60), channel_id=1, source_target_pairs={{4,0},{8,4},{12,8},{16,12},{20,16},{24,20},{28,24},{32,28},{36,32}... | collective-permute-start | bytes 49160 | tf_op jit(solution)/shard_map/ppermute | solution.py:17
  73.1 1.4 collective-permute-done.9
  74.5 1.9 %collective-permute-start.10 = (f32[1,18,256]{2,1,0:T(8,128)S(1)}, f32[1,18,256]{2,1,0:T(8,128)S(1)}, u32[]{:S(2)}, u32[]{:S(2)}) collective-permute-start(f32[1,18,256]{2,1,0:T(8,128)S(1)} %get-tuple-element.42), channel_id=1, source_target_pairs={{1,0},{2,1},{3,2},{5,4},{6,5},{7,6},{9,8},{10,9},{11,10},{13,12},{... | collective-permute-start | bytes 55304 | tf_op jit(solution)/shard_map/ppermute | solution.py:17
  76.5 2.4 %collective-permute-start.11 = (f32[1,18,256]{2,1,0:T(8,128)S(1)}, f32[1,18,256]{2,1,0:T(8,128)S(1)}, u32[]{:S(2)}, u32[]{:S(2)}) collective-permute-start(f32[1,18,256]{2,1,0:T(8,128)S(1)} %get-tuple-element.43), channel_id=1, source_target_pairs={{0,1},{1,2},{2,3},{4,5},{5,6},{6,7},{8,9},{9,10},{10,11},{12,13},{... | collective-permute-start | bytes 55304 | tf_op jit(solution)/shard_map/ppermute | solution.py:14
  78.9 0.1 fusion.117
  79.0 2.6 %collective-permute-done.11 = f32[1,18,256]{2,1,0:T(8,128)S(1)} collective-permute-done((f32[1,18,256]{2,1,0:T(8,128)S(1)}, f32[1,18,256]{2,1,0:T(8,128)S(1)}, u32[]{:S(2)}, u32[]{:S(2)}) %collective-permute-start.11) | collective-permute-done | bytes 18464 | tf_op jit(solution)/shard_map/ppermute | solution.py:14
  81.6 0.4 fusion.67
  82.1 1.9 %collective-permute-start.12 = (f32[16,1,256]{2,1,0:T(1,128)S(1)}, f32[16,1,256]{2,1,0:T(1,128)S(1)}, u32[]{:S(2)}, u32[]{:S(2)}) collective-permute-start(f32[16,1,256]{2,1,0:T(1,128)S(1)} %get-tuple-element.57), channel_id=1, source_target_pairs={{0,4},{4,8},{8,12},{12,16},{16,20},{20,24},{24,28},{28,32},{32,36}... | collective-permute-start | bytes 49160 | tf_op jit(solution)/shard_map/ppermute | solution.py:14
  84.0 8.7 %collective-permute-start.13 = (f32[16,1,256]{2,1,0:T(1,128)S(1)}, f32[16,1,256]{2,1,0:T(1,128)S(1)}, u32[]{:S(2)}, u32[]{:S(2)}) collective-permute-start(f32[16,1,256]{2,1,0:T(1,128)S(1)} %get-tuple-element.56), channel_id=1, source_target_pairs={{4,0},{8,4},{12,8},{16,12},{20,16},{24,20},{28,24},{32,28},{36,32}... | collective-permute-start | bytes 49160 | tf_op jit(solution)/shard_map/ppermute | solution.py:17
  92.7 1.4 collective-permute-done.13
  94.2 1.9 %collective-permute-start.14 = (f32[1,18,256]{2,1,0:T(8,128)S(1)}, f32[1,18,256]{2,1,0:T(8,128)S(1)}, u32[]{:S(2)}, u32[]{:S(2)}) collective-permute-start(f32[1,18,256]{2,1,0:T(8,128)S(1)} %get-tuple-element.40), channel_id=1, source_target_pairs={{1,0},{2,1},{3,2},{5,4},{6,5},{7,6},{9,8},{10,9},{11,10},{13,12},{... | collective-permute-start | bytes 55304 | tf_op jit(solution)/shard_map/ppermute | solution.py:17
  96.1 2.4 %collective-permute-start.15 = (f32[1,18,256]{2,1,0:T(8,128)S(1)}, f32[1,18,256]{2,1,0:T(8,128)S(1)}, u32[]{:S(2)}, u32[]{:S(2)}) collective-permute-start(f32[1,18,256]{2,1,0:T(8,128)S(1)} %get-tuple-element.41), channel_id=1, source_target_pairs={{0,1},{1,2},{2,3},{4,5},{5,6},{6,7},{8,9},{9,10},{10,11},{12,13},{... | collective-permute-start | bytes 55304 | tf_op jit(solution)/shard_map/ppermute | solution.py:14
  98.5 0.1 fusion.115
  98.7 2.6 %collective-permute-done.15 = f32[1,18,256]{2,1,0:T(8,128)S(1)} collective-permute-done((f32[1,18,256]{2,1,0:T(8,128)S(1)}, f32[1,18,256]{2,1,0:T(8,128)S(1)}, u32[]{:S(2)}, u32[]{:S(2)}) %collective-permute-start.15) | collective-permute-done | bytes 18464 | tf_op jit(solution)/shard_map/ppermute | solution.py:14
  101.2 0.4 fusion.50
  101.7 1.9 %collective-permute-start.16 = (f32[16,1,256]{2,1,0:T(1,128)S(1)}, f32[16,1,256]{2,1,0:T(1,128)S(1)}, u32[]{:S(2)}, u32[]{:S(2)}) collective-permute-start(f32[16,1,256]{2,1,0:T(1,128)S(1)} %get-tuple-element.53), channel_id=1, source_target_pairs={{0,4},{4,8},{8,12},{12,16},{16,20},{20,24},{24,28},{28,32},{32,36}... | collective-permute-start | bytes 49160 | tf_op jit(solution)/shard_map/ppermute | solution.py:14
  103.6 8.7 %collective-permute-start.17 = (f32[16,1,256]{2,1,0:T(1,128)S(1)}, f32[16,1,256]{2,1,0:T(1,128)S(1)}, u32[]{:S(2)}, u32[]{:S(2)}) collective-permute-start(f32[16,1,256]{2,1,0:T(1,128)S(1)} %get-tuple-element.52), channel_id=1, source_target_pairs={{4,0},{8,4},{12,8},{16,12},{20,16},{24,20},{28,24},{32,28},{36,32}... | collective-permute-start | bytes 49160 | tf_op jit(solution)/shard_map/ppermute | solution.py:17
  112.4 1.4 collective-permute-done.17
  113.8 1.9 %collective-permute-start.18 = (f32[1,18,256]{2,1,0:T(8,128)S(1)}, f32[1,18,256]{2,1,0:T(8,128)S(1)}, u32[]{:S(2)}, u32[]{:S(2)}) collective-permute-start(f32[1,18,256]{2,1,0:T(8,128)S(1)} %get-tuple-element.38), channel_id=1, source_target_pairs={{1,0},{2,1},{3,2},{5,4},{6,5},{7,6},{9,8},{10,9},{11,10},{13,12},{... | collective-permute-start | bytes 55304 | tf_op jit(solution)/shard_map/ppermute | solution.py:17
  115.7 2.4 %collective-permute-start.19 = (f32[1,18,256]{2,1,0:T(8,128)S(1)}, f32[1,18,256]{2,1,0:T(8,128)S(1)}, u32[]{:S(2)}, u32[]{:S(2)}) collective-permute-start(f32[1,18,256]{2,1,0:T(8,128)S(1)} %get-tuple-element.39), channel_id=1, source_target_pairs={{0,1},{1,2},{2,3},{4,5},{5,6},{6,7},{8,9},{9,10},{10,11},{12,13},{... | collective-permute-start | bytes 55304 | tf_op jit(solution)/shard_map/ppermute | solution.py:14
  118.1 0.1 fusion.113
  118.3 2.6 %collective-permute-done.19 = f32[1,18,256]{2,1,0:T(8,128)S(1)} collective-permute-done((f32[1,18,256]{2,1,0:T(8,128)S(1)}, f32[1,18,256]{2,1,0:T(8,128)S(1)}, u32[]{:S(2)}, u32[]{:S(2)}) %collective-permute-start.19) | collective-permute-done | bytes 18464 | tf_op jit(solution)/shard_map/ppermute | solution.py:14
  120.9 0.4 fusion.33
  121.4 1.9 %collective-permute-start.20 = (f32[16,1,256]{2,1,0:T(1,128)S(1)}, f32[16,1,256]{2,1,0:T(1,128)S(1)}, u32[]{:S(2)}, u32[]{:S(2)}) collective-permute-start(f32[16,1,256]{2,1,0:T(1,128)S(1)} %get-tuple-element.48), channel_id=1, source_target_pairs={{0,4},{4,8},{8,12},{12,16},{16,20},{20,24},{24,28},{28,32},{32,36}... | collective-permute-start | bytes 49160 | tf_op jit(solution)/shard_map/ppermute | solution.py:14
  123.3 8.7 %collective-permute-start.21 = (f32[16,1,256]{2,1,0:T(1,128)S(1)}, f32[16,1,256]{2,1,0:T(1,128)S(1)}, u32[]{:S(2)}, u32[]{:S(2)}) collective-permute-start(f32[16,1,256]{2,1,0:T(1,128)S(1)} %get-tuple-element.49), channel_id=1, source_target_pairs={{4,0},{8,4},{12,8},{16,12},{20,16},{24,20},{28,24},{32,28},{36,32}... | collective-permute-start | bytes 49160 | tf_op jit(solution)/shard_map/ppermute | solution.py:17
  132.0 0.1 fusion.109
  132.2 1.3 collective-permute-done.21
  133.4 1.9 %collective-permute-start.22 = (f32[1,18,256]{2,1,0:T(8,128)S(1)}, f32[1,18,256]{2,1,0:T(8,128)S(1)}, u32[]{:S(2)}, u32[]{:S(2)}) collective-permute-start(f32[1,18,256]{2,1,0:T(8,128)S(1)} %get-tuple-element.37), channel_id=1, source_target_pairs={{1,0},{2,1},{3,2},{5,4},{6,5},{7,6},{9,8},{10,9},{11,10},{13,12},{... | collective-permute-start | bytes 55304 | tf_op jit(solution)/shard_map/ppermute | solution.py:17
  135.4 2.4 %collective-permute-start.23 = (f32[1,18,256]{2,1,0:T(8,128)S(1)}, f32[1,18,256]{2,1,0:T(8,128)S(1)}, u32[]{:S(2)}, u32[]{:S(2)}) collective-permute-start(f32[1,18,256]{2,1,0:T(8,128)S(1)} %get-tuple-element.36), channel_id=1, source_target_pairs={{0,1},{1,2},{2,3},{4,5},{5,6},{6,7},{8,9},{9,10},{10,11},{12,13},{... | collective-permute-start | bytes 55304 | tf_op jit(solution)/shard_map/ppermute | solution.py:14
  137.8 0.1 fusion.111
  138.0 2.5 %collective-permute-done.23 = f32[1,18,256]{2,1,0:T(8,128)S(1)} collective-permute-done((f32[1,18,256]{2,1,0:T(8,128)S(1)}, f32[1,18,256]{2,1,0:T(8,128)S(1)}, u32[]{:S(2)}, u32[]{:S(2)}) %collective-permute-start.23) | collective-permute-done | bytes 18464 | tf_op jit(solution)/shard_map/ppermute | solution.py:14
  140.5 1.1 add_subtract_fusion
  141.6 1.6 %fusion.103 = (f32[16,16,256]{2,1,0:T(8,128)}, f32[16,16,256]{2,1,0:T(8,128)}) fusion(f32[16,16,256]{2,1,0:T(8,128)S(1)} %copy-done.5, f32[16,16,256]{2,1,0:T(8,128)S(1)} %copy-done.4, f32[16,16,256]{2,1,0:T(8,128)S(1)} %copy-done.6, f32[16,16,255]{2,1,0:T(8,128)S(1)} %get-tuple-element.33, f32[16,16,256]{2,1,0:T(8,128)S(1)} %get-tuple-element.13, ...), kind=kLoop, calls=%fused_computation.208 | loop fusion | flops 4521984 | bytes 5832704 | tf_op jit(solution)/shard_map/max | solution.py:136
  (67 shorter events, 0.8 us)
Async XLA Ops:
  0.6 18.3 %copy-start = (f32[16,16,256]{2,1,0:T(8,128)S(1)}, f32[16,16,256]{2,1,0:T(8,128)}, u32[]{:S(2)}) copy-start(f32[16,16,256]{2,1,0:T(8,128)} %param.10) | copy-start | bytes 786436
  1.8 28.3 %copy-start.3 = (f32[3,16,16,256]{3,2,1,0:T(8,128)S(1)}, f32[3,16,16,256]{3,2,1,0:T(8,128)}, u32[]{:S(2)}) copy-start(f32[3,16,16,256]{3,2,1,0:T(8,128)} %param.15) | copy-start | bytes 2359300
  1.8 28.4 %copy-start.10 = (s32[32,16]{0,1:T(8,128)S(1)}, s32[32,16]{0,1:T(8,128)}, u32[]{:S(2)}) copy-start(s32[32,16]{0,1:T(8,128)} %param.16) | copy-start | bytes 6148
  3.9 43.8 %collective-permute-start = (f32[4,16,1,256]{3,2,1,0:T(1,128)}, f32[4,16,1,256]{3,2,1,0:T(1,128)S(1)}, u32[]{:S(2)}, u32[]{:S(2)}) collective-permute-start(f32[4,16,1,256]{3,2,1,0:T(1,128)} %get-tuple-element.27), channel_id=1, source_target_pairs={{0,4},{4,8},{8,12},{12,16},{16,20},{20,24},{24,28},{28,32},{32,36}... | collective-permute-start | bytes 196616 | tf_op jit(solution)/shard_map/ppermute | solution.py:14
  7.7 40.0 %collective-permute-start.1 = (f32[4,16,1,256]{3,2,1,0:T(1,128)}, f32[4,16,1,256]{3,2,1,0:T(1,128)S(1)}, u32[]{:S(2)}, u32[]{:S(2)}) collective-permute-start(f32[4,16,1,256]{3,2,1,0:T(1,128)} %get-tuple-element.28), channel_id=1, source_target_pairs={{4,0},{8,4},{12,8},{16,12},{20,16},{24,20},{28,24},{32,28},{36,32}... | collective-permute-start | bytes 196616 | tf_op jit(solution)/shard_map/ppermute | solution.py:17
  19.6 33.8 %collective-permute-start.4 = (f32[16,1,256]{2,1,0:T(1,128)}, f32[16,1,256]{2,1,0:T(1,128)}, u32[]{:S(2)}, u32[]{:S(2)}) collective-permute-start(f32[16,1,256]{2,1,0:T(1,128)} %get-tuple-element.65), channel_id=1, source_target_pairs={{0,4},{4,8},{8,12},{12,16},{16,20},{20,24},{24,28},{28,32},{32,36}... | collective-permute-start | bytes 49160 | tf_op jit(solution)/shard_map/ppermute | solution.py:14
  21.5 31.9 %collective-permute-start.5 = (f32[16,1,256]{2,1,0:T(1,128)}, f32[16,1,256]{2,1,0:T(1,128)}, u32[]{:S(2)}, u32[]{:S(2)}) collective-permute-start(f32[16,1,256]{2,1,0:T(1,128)} %get-tuple-element.64), channel_id=1, source_target_pairs={{4,0},{8,4},{12,8},{16,12},{20,16},{24,20},{28,24},{32,28},{36,32}... | collective-permute-start | bytes 49160 | tf_op jit(solution)/shard_map/ppermute | solution.py:17
  30.2 0.7 copy-start.7
  34.5 3.3 %copy-start.11 = (f32[32,16]{0,1:T(8,128)S(1)}, f32[32,16]{0,1:T(8,128)}, u32[]{:S(2)}) copy-start(f32[32,16]{0,1:T(8,128)} %param.17) | copy-start | bytes 6148
  34.5 3.4 %copy-start.8 = (s32[32,16]{1,0:T(8,128)S(1)}, s32[32,16]{1,0:T(8,128)}, u32[]{:S(2)}) copy-start(s32[32,16]{1,0:T(8,128)} %copy-done.7) | copy-start | bytes 6148
  34.5 9.2 %copy-start.13 = (f32[32]{0:T(128)S(1)}, f32[32]{0:T(128)}, u32[]{:S(2)}) copy-start(f32[32]{0:T(128)} %param.19) | copy-start | bytes 388
  34.5 9.1 %copy-start.14 = (s32[32]{0:T(128)S(1)}, s32[32]{0:T(128)}, u32[]{:S(2)}) copy-start(s32[32]{0:T(128)} %param.18) | copy-start | bytes 388
  34.5 9.3 %copy-start.9 = (s32[32,16]{1,0:T(8,128)S(1)}, s32[32,16]{1,0:T(8,128)}, u32[]{:S(2)}) copy-start(s32[32,16]{1,0:T(8,128)} %get-tuple-element.20) | copy-start | bytes 6148
  43.6 15.1 %copy-start.12 = (f32[32]{0:T(128)}, f32[32]{0:T(128)S(1)}, u32[]{:S(2)}) copy-start(f32[32]{0:T(128)S(1)} %compare_select_fusion.2) | copy-start | bytes 388
  47.8 10.6 %collective-permute-start.2 = (f32[4,1,18,256]{3,2,1,0:T(8,128)S(1)}, f32[4,1,18,256]{3,2,1,0:T(8,128)S(1)}, u32[]{:S(2)}, u32[]{:S(2)}) collective-permute-start(f32[4,1,18,256]{3,2,1,0:T(8,128)S(1)} %get-tuple-element.25), channel_id=1, source_target_pairs={{0,1},{1,2},{2,3},{4,5},{5,6},{6,7},{8,9},{9,10},{10,11},{12,13},{... | collective-permute-start | bytes 221192 | tf_op jit(solution)/shard_map/ppermute | solution.py:14
  49.8 8.6 %collective-permute-start.3 = (f32[4,1,18,256]{3,2,1,0:T(8,128)S(1)}, f32[4,1,18,256]{3,2,1,0:T(8,128)S(1)}, u32[]{:S(2)}, u32[]{:S(2)}) collective-permute-start(f32[4,1,18,256]{3,2,1,0:T(8,128)S(1)} %get-tuple-element.26), channel_id=1, source_target_pairs={{1,0},{2,1},{3,2},{5,4},{6,5},{7,6},{9,8},{10,9},{11,10},{13,12},{... | collective-permute-start | bytes 221192 | tf_op jit(solution)/shard_map/ppermute | solution.py:17
  54.1 4.9 %collective-permute-start.6 = (f32[1,18,256]{2,1,0:T(8,128)S(1)}, f32[1,18,256]{2,1,0:T(8,128)S(1)}, u32[]{:S(2)}, u32[]{:S(2)}) collective-permute-start(f32[1,18,256]{2,1,0:T(8,128)S(1)} %get-tuple-element.44), channel_id=1, source_target_pairs={{1,0},{2,1},{3,2},{5,4},{6,5},{7,6},{9,8},{10,9},{11,10},{13,12},{... | collective-permute-start | bytes 55304 | tf_op jit(solution)/shard_map/ppermute | solution.py:17
  56.0 5.1 %collective-permute-start.7 = (f32[1,18,256]{2,1,0:T(8,128)S(1)}, f32[1,18,256]{2,1,0:T(8,128)S(1)}, u32[]{:S(2)}, u32[]{:S(2)}) collective-permute-start(f32[1,18,256]{2,1,0:T(8,128)S(1)} %get-tuple-element.45), channel_id=1, source_target_pairs={{0,1},{1,2},{2,3},{4,5},{5,6},{6,7},{8,9},{9,10},{10,11},{12,13},{... | collective-permute-start | bytes 55304 | tf_op jit(solution)/shard_map/ppermute | solution.py:14
  58.7 2.4 %copy-start.2 = (f32[16,16,256]{2,1,0:T(8,128)S(1)}, f32[16,16,256]{2,1,0:T(8,128)}, u32[]{:S(2)}) copy-start(f32[16,16,256]{2,1,0:T(8,128)} %param.13) | copy-start | bytes 786436
  62.7 10.4 %collective-permute-start.8 = (f32[16,1,256]{2,1,0:T(1,128)S(1)}, f32[16,1,256]{2,1,0:T(1,128)S(1)}, u32[]{:S(2)}, u32[]{:S(2)}) collective-permute-start(f32[16,1,256]{2,1,0:T(1,128)S(1)} %get-tuple-element.61), channel_id=1, source_target_pairs={{0,4},{4,8},{8,12},{12,16},{16,20},{20,24},{24,28},{28,32},{32,36}... | collective-permute-start | bytes 49160 | tf_op jit(solution)/shard_map/ppermute | solution.py:14
  64.7 9.9 %collective-permute-start.9 = (f32[16,1,256]{2,1,0:T(1,128)S(1)}, f32[16,1,256]{2,1,0:T(1,128)S(1)}, u32[]{:S(2)}, u32[]{:S(2)}) collective-permute-start(f32[16,1,256]{2,1,0:T(1,128)S(1)} %get-tuple-element.60), channel_id=1, source_target_pairs={{4,0},{8,4},{12,8},{16,12},{20,16},{24,20},{28,24},{32,28},{36,32}... | collective-permute-start | bytes 49160 | tf_op jit(solution)/shard_map/ppermute | solution.py:17
  74.5 4.5 %collective-permute-start.10 = (f32[1,18,256]{2,1,0:T(8,128)S(1)}, f32[1,18,256]{2,1,0:T(8,128)S(1)}, u32[]{:S(2)}, u32[]{:S(2)}) collective-permute-start(f32[1,18,256]{2,1,0:T(8,128)S(1)} %get-tuple-element.42), channel_id=1, source_target_pairs={{1,0},{2,1},{3,2},{5,4},{6,5},{7,6},{9,8},{10,9},{11,10},{13,12},{... | collective-permute-start | bytes 55304 | tf_op jit(solution)/shard_map/ppermute | solution.py:17
  76.5 5.1 %collective-permute-start.11 = (f32[1,18,256]{2,1,0:T(8,128)S(1)}, f32[1,18,256]{2,1,0:T(8,128)S(1)}, u32[]{:S(2)}, u32[]{:S(2)}) collective-permute-start(f32[1,18,256]{2,1,0:T(8,128)S(1)} %get-tuple-element.43), channel_id=1, source_target_pairs={{0,1},{1,2},{2,3},{4,5},{5,6},{6,7},{8,9},{9,10},{10,11},{12,13},{... | collective-permute-start | bytes 55304 | tf_op jit(solution)/shard_map/ppermute | solution.py:14
  82.1 10.7 %collective-permute-start.12 = (f32[16,1,256]{2,1,0:T(1,128)S(1)}, f32[16,1,256]{2,1,0:T(1,128)S(1)}, u32[]{:S(2)}, u32[]{:S(2)}) collective-permute-start(f32[16,1,256]{2,1,0:T(1,128)S(1)} %get-tuple-element.57), channel_id=1, source_target_pairs={{0,4},{4,8},{8,12},{12,16},{16,20},{20,24},{24,28},{28,32},{32,36}... | collective-permute-start | bytes 49160 | tf_op jit(solution)/shard_map/ppermute | solution.py:14
  84.0 10.1 %collective-permute-start.13 = (f32[16,1,256]{2,1,0:T(1,128)S(1)}, f32[16,1,256]{2,1,0:T(1,128)S(1)}, u32[]{:S(2)}, u32[]{:S(2)}) collective-permute-start(f32[16,1,256]{2,1,0:T(1,128)S(1)} %get-tuple-element.56), channel_id=1, source_target_pairs={{4,0},{8,4},{12,8},{16,12},{20,16},{24,20},{28,24},{32,28},{36,32}... | collective-permute-start | bytes 49160 | tf_op jit(solution)/shard_map/ppermute | solution.py:17
  94.2 4.5 %collective-permute-start.14 = (f32[1,18,256]{2,1,0:T(8,128)S(1)}, f32[1,18,256]{2,1,0:T(8,128)S(1)}, u32[]{:S(2)}, u32[]{:S(2)}) collective-permute-start(f32[1,18,256]{2,1,0:T(8,128)S(1)} %get-tuple-element.40), channel_id=1, source_target_pairs={{1,0},{2,1},{3,2},{5,4},{6,5},{7,6},{9,8},{10,9},{11,10},{13,12},{... | collective-permute-start | bytes 55304 | tf_op jit(solution)/shard_map/ppermute | solution.py:17
  96.1 5.1 %collective-permute-start.15 = (f32[1,18,256]{2,1,0:T(8,128)S(1)}, f32[1,18,256]{2,1,0:T(8,128)S(1)}, u32[]{:S(2)}, u32[]{:S(2)}) collective-permute-start(f32[1,18,256]{2,1,0:T(8,128)S(1)} %get-tuple-element.41), channel_id=1, source_target_pairs={{0,1},{1,2},{2,3},{4,5},{5,6},{6,7},{8,9},{9,10},{10,11},{12,13},{... | collective-permute-start | bytes 55304 | tf_op jit(solution)/shard_map/ppermute | solution.py:14
  101.7 10.7 %collective-permute-start.16 = (f32[16,1,256]{2,1,0:T(1,128)S(1)}, f32[16,1,256]{2,1,0:T(1,128)S(1)}, u32[]{:S(2)}, u32[]{:S(2)}) collective-permute-start(f32[16,1,256]{2,1,0:T(1,128)S(1)} %get-tuple-element.53), channel_id=1, source_target_pairs={{0,4},{4,8},{8,12},{12,16},{16,20},{20,24},{24,28},{28,32},{32,36}... | collective-permute-start | bytes 49160 | tf_op jit(solution)/shard_map/ppermute | solution.py:14
  103.6 10.1 %collective-permute-start.17 = (f32[16,1,256]{2,1,0:T(1,128)S(1)}, f32[16,1,256]{2,1,0:T(1,128)S(1)}, u32[]{:S(2)}, u32[]{:S(2)}) collective-permute-start(f32[16,1,256]{2,1,0:T(1,128)S(1)} %get-tuple-element.52), channel_id=1, source_target_pairs={{4,0},{8,4},{12,8},{16,12},{20,16},{24,20},{28,24},{32,28},{36,32}... | collective-permute-start | bytes 49160 | tf_op jit(solution)/shard_map/ppermute | solution.py:17
  113.8 4.5 %collective-permute-start.18 = (f32[1,18,256]{2,1,0:T(8,128)S(1)}, f32[1,18,256]{2,1,0:T(8,128)S(1)}, u32[]{:S(2)}, u32[]{:S(2)}) collective-permute-start(f32[1,18,256]{2,1,0:T(8,128)S(1)} %get-tuple-element.38), channel_id=1, source_target_pairs={{1,0},{2,1},{3,2},{5,4},{6,5},{7,6},{9,8},{10,9},{11,10},{13,12},{... | collective-permute-start | bytes 55304 | tf_op jit(solution)/shard_map/ppermute | solution.py:17
  115.7 5.1 %collective-permute-start.19 = (f32[1,18,256]{2,1,0:T(8,128)S(1)}, f32[1,18,256]{2,1,0:T(8,128)S(1)}, u32[]{:S(2)}, u32[]{:S(2)}) collective-permute-start(f32[1,18,256]{2,1,0:T(8,128)S(1)} %get-tuple-element.39), channel_id=1, source_target_pairs={{0,1},{1,2},{2,3},{4,5},{5,6},{6,7},{8,9},{9,10},{10,11},{12,13},{... | collective-permute-start | bytes 55304 | tf_op jit(solution)/shard_map/ppermute | solution.py:14
  121.3 20.3 %copy-start.1 = (f32[16,16,256]{2,1,0:T(8,128)}, f32[16,16,256]{2,1,0:T(8,128)S(1)}, u32[]{:S(2)}) copy-start(f32[16,16,256]{2,1,0:T(8,128)S(1)} %fusion.33) | copy-start | bytes 786436
  121.4 10.8 %collective-permute-start.20 = (f32[16,1,256]{2,1,0:T(1,128)S(1)}, f32[16,1,256]{2,1,0:T(1,128)S(1)}, u32[]{:S(2)}, u32[]{:S(2)}) collective-permute-start(f32[16,1,256]{2,1,0:T(1,128)S(1)} %get-tuple-element.48), channel_id=1, source_target_pairs={{0,4},{4,8},{8,12},{12,16},{16,20},{20,24},{24,28},{28,32},{32,36}... | collective-permute-start | bytes 49160 | tf_op jit(solution)/shard_map/ppermute | solution.py:14
  123.3 10.1 %collective-permute-start.21 = (f32[16,1,256]{2,1,0:T(1,128)S(1)}, f32[16,1,256]{2,1,0:T(1,128)S(1)}, u32[]{:S(2)}, u32[]{:S(2)}) collective-permute-start(f32[16,1,256]{2,1,0:T(1,128)S(1)} %get-tuple-element.49), channel_id=1, source_target_pairs={{4,0},{8,4},{12,8},{16,12},{20,16},{24,20},{28,24},{32,28},{36,32}... | collective-permute-start | bytes 49160 | tf_op jit(solution)/shard_map/ppermute | solution.py:17
  133.4 4.5 %collective-permute-start.22 = (f32[1,18,256]{2,1,0:T(8,128)S(1)}, f32[1,18,256]{2,1,0:T(8,128)S(1)}, u32[]{:S(2)}, u32[]{:S(2)}) collective-permute-start(f32[1,18,256]{2,1,0:T(8,128)S(1)} %get-tuple-element.37), channel_id=1, source_target_pairs={{1,0},{2,1},{3,2},{5,4},{6,5},{7,6},{9,8},{10,9},{11,10},{13,12},{... | collective-permute-start | bytes 55304 | tf_op jit(solution)/shard_map/ppermute | solution.py:17
  135.4 5.1 %collective-permute-start.23 = (f32[1,18,256]{2,1,0:T(8,128)S(1)}, f32[1,18,256]{2,1,0:T(8,128)S(1)}, u32[]{:S(2)}, u32[]{:S(2)}) collective-permute-start(f32[1,18,256]{2,1,0:T(8,128)S(1)} %get-tuple-element.36), channel_id=1, source_target_pairs={{0,1},{1,2},{2,3},{4,5},{5,6},{6,7},{8,9},{9,10},{10,11},{12,13},{... | collective-permute-start | bytes 55304 | tf_op jit(solution)/shard_map/ppermute | solution.py:14
  137.9 3.7 %copy-start.4 = (f32[16,16,256]{2,1,0:T(8,128)S(1)}, f32[16,16,256]{2,1,0:T(8,128)}, u32[]{:S(2)}) copy-start(f32[16,16,256]{2,1,0:T(8,128)} %param.11) | copy-start | bytes 786436
  137.9 3.7 %copy-start.5 = (f32[16,16,256]{2,1,0:T(8,128)S(1)}, f32[16,16,256]{2,1,0:T(8,128)}, u32[]{:S(2)}) copy-start(f32[16,16,256]{2,1,0:T(8,128)} %param.12) | copy-start | bytes 786436
  137.9 3.7 %copy-start.6 = (f32[16,16,256]{2,1,0:T(8,128)S(1)}, f32[16,16,256]{2,1,0:T(8,128)}, u32[]{:S(2)}) copy-start(f32[16,16,256]{2,1,0:T(8,128)} %param.14) | copy-start | bytes 786436
where the time goes:
time: 144 us; the launch traced here: 143 us
  starting transfers between devices  94.8 us (66%)
  waiting for transfers between devices  18 us (12%)
  other arithmetic  13.2 us (9%)
  local copies, waits for them, and re-layouts  10.2 us (7%)
  blocking collectives  5.69 us (4%)
    ppermute x12, starting transfers between devices, padded(): lax.ppermute(lax.slice_in_dim(block, 0, width, axis=dim), axis, backward)  67.4 us
    ppermute x12, starting transfers between devices, padded(): lax.ppermute(lax.slice_in_dim(block, block.shape[dim] - width, None, axis...  27.5 us
    ppermute x12, waiting for transfers between devices, padded(): lax.ppermute(lax.slice_in_dim(block, block.shape[dim] - width, None, axis...  12.5 us
    psum x1, blocking collectives, body(): sum_p, sum_w = lax.psum((part_p, part_w), 'gz')  5.69 us
    ppermute x12, waiting for transfers between devices, padded(): lax.ppermute(lax.slice_in_dim(block, 0, width, axis=dim), axis, backward)  5.52 us
    scatter-add x1, other arithmetic, body(): source = jnp.zeros((cells,), jnp.float32).at[safe_index.reshape(-1)].add(...  3.69 us
    gather x2, local copies, waits for them, and re-layouts, body(): cell_p = flat_pressure[safe_index]  3.22 us
    gather x2, local copies, waits for them, and re-layouts, body(): weight = jnp.where(inside, perf_index * total.reshape(-1)[safe_index], 0.0)  3.22 us
  transfers between devices with their start and end apart: 24, of which 9 were waited for; matrix products, arithmetic and copies ran while one was open for 10% of the time, Pallas kernels for 0%

commit v1 on v0

v1 whole, which is shorter than its diff:
```python
import functools

import jax
import jax.numpy as jnp
from jax import lax
from jax.experimental import pallas as pl
from jax.experimental.pallas import tpu as pltpu
from jax.sharding import PartitionSpec as P

L = 16
R = 16
C = 256
H = 4
X = L + 2 * H
WELLS = 32
NP = 16
GROUPS = WELLS * NP // 128
HI = L
LO = L + H
AP, ATO, AST, AT0, AT1, AT2 = range(6)
PACKED = (AP, AST, AT0, AT1, AT2)
RAW = 4 * len(PACKED)
PAIRS = ((AP, ATO), (AST, AT0), (AT1, AT2))
MESH = pl.DeviceIdType.MESH
F32 = jnp.float32
BF16 = jnp.bfloat16
VMEM_LIMIT = 26 * 2**20


def mobility(sat, history):
    trapped = history / (1.0 + 1.5 * history)
    excess = jnp.maximum(sat - trapped, 0.0)
    free_gas = 0.5 * (excess + jnp.sqrt(excess * excess + excess / 0.375))
    relperm = jnp.where(sat < history, free_gas * free_gas, sat * sat)
    gas = relperm / 0.5
    total = (1.0 - sat) * (1.0 - sat) + gas
    return (total, gas / total)


def split(values):
    high = values.astype(BF16)
    low = (values - high.astype(F32)).astype(BF16)
    return high, low


def four(row):
    return jnp.concatenate([row, row, row, row], axis=1)


def lane_groups(table):
    wide = four(table)
    place = lax.broadcasted_iota(jnp.int32, (1, 128), 1) // WELLS
    rows = []
    for g in range(GROUPS):
        row = wide[4 * g : 4 * g + 1]
        for k in range(1, 4):
            row = jnp.where(place == k, wide[4 * g + k : 4 * g + k + 1], row)
        rows.append(row)
    return rows


def cell_parts(cell, gz):
    layer = lax.shift_right_logical(cell, 12) - gz * L
    row = lax.shift_right_logical(cell, 8) & (R - 1)
    column = cell & (C - 1)
    index = jnp.where(layer < 0, layer + X, layer)
    inside = (layer >= -H) & (layer < L + H)
    return index, row, column, inside


def one_hot(size, target):
    return jnp.where(lax.broadcasted_iota(jnp.int32, (size, 128), 0) == target, 1.0, 0.0)


def own_rows(cell, gz):
    index, row, _, inside = cell_parts(cell, gz)
    return jnp.where(inside, index * R + row, -1)


def side_rows(cell, gz, side):
    index, row, _, inside = cell_parts(cell, gz)
    if side == 0:
        inside = inside & (row >= R - H)
        place = index * 8 + row - 8
    else:
        inside = inside & (row < H)
        place = index * 8 + row
    return jnp.where(inside, place, -1)


def scatter(rows, values):
    high, low = split(values)
    dims = (((1,), (1,)), ((), ()))
    return lax.dot_general(rows, high, dims, preferred_element_type=F32) + lax.dot_general(
        rows, low, dims, preferred_element_type=F32
    )


def column_values(columns, values):
    place = lax.broadcasted_iota(jnp.int32, (C, 128), 0)
    return jnp.concatenate(
        [jnp.where(place == c, v, 0.0) for c, v in zip(columns, values)], axis=1
    )


def exchange(
    count_x,
    count_z,
    p_in,
    sat_in,
    hist_in,
    sto_in,
    vol_in,
    tr_in,
    pc_in,
    pi_in,
    ctl_in,
    tgt_in,
    ext,
    frac,
    local,
    index_sum,
    own_hot,
    side_hot,
    cols,
    idxs,
    edge_x,
    edge_z,
    tiles,
    raw_out,
    raw_in,
    cmp_out,
    cmp_in,
    corner_out,
    corner_in,
    edge_out,
    tile_out,
    pc,
    pi,
    ctl,
    tgt,
    load_sem,
    send_sem,
    recv_sem,
):
    gx, gz = lax.axis_index("gx"), lax.axis_index("gz")
    has = {
        ("x", 0): gx > 0,
        ("x", 1): gx < count_x - 1,
        ("z", 0): gz > 0,
        ("z", 1): gz < count_z - 1,
    }
    step = (-1, 1)

    barrier = pltpu.get_barrier_semaphore()

    def signal_column(x):
        def one(z, carry):
            pl.semaphore_signal(barrier, inc=1, device_id=(x, z), device_id_type=MESH)
            return carry

        return one

    def others(z, carry):
        @pl.when(z != gz)
        def _():
            pl.semaphore_signal(barrier, inc=1, device_id=(gx, z), device_id_type=MESH)

        return carry

    for s in (0, 1):

        @pl.when(has["x", s])
        def _():
            lax.fori_loop(0, count_z, signal_column(gx + step[s]), 0)

    lax.fori_loop(0, count_z, others, 0)

    own = pl.ds(0, L)
    loads = [
        pltpu.make_async_copy(pc_in, pc.at[0], load_sem.at[0]),
        pltpu.make_async_copy(pi_in, pi.at[0], load_sem.at[1]),
        pltpu.make_async_copy(ctl_in, ctl, load_sem.at[2]),
        pltpu.make_async_copy(tgt_in, tgt, load_sem.at[3]),
        pltpu.make_async_copy(p_in, ext.at[AP, own, own], load_sem.at[4]),
        pltpu.make_async_copy(sto_in, ext.at[AST, own, own], load_sem.at[5]),
        pltpu.make_async_copy(tr_in, ext.at[pl.ds(AT0, 3), own, own], load_sem.at[6]),
        pltpu.make_async_copy(sat_in, local.at[0], load_sem.at[7]),
        pltpu.make_async_copy(hist_in, local.at[1], load_sem.at[8]),
        pltpu.make_async_copy(vol_in, local.at[2], load_sem.at[9]),
    ]
    for copy in loads:
        copy.start()

    for s in (0, 1):
        z0 = LO if s == 0 else HI

        @pl.when(jnp.logical_not(has["x", s]))
        def _():
            raw_in[s] = jnp.zeros((RAW, L, C), F32)
            raw_in[s, 4:8] = jnp.ones((4, L, C), F32)
            cmp_in[s] = jnp.zeros((5, L, C), F32)
            edge_x[s] = jnp.zeros((2, L, C), F32)
            pc[1 + s] = jnp.full((NP, WELLS), 1 << 30, jnp.int32)
            pi[1 + s] = jnp.zeros((NP, WELLS), F32)
            tiles[4 * (2 * s) : 4 * (2 * s) + 4] = jnp.ones((4, 8, 128), F32)

        @pl.when(jnp.logical_not(has["z", s]))
        def _():
            for a in range(6):
                fill = jnp.ones if a == AST else jnp.zeros
                ext[a, z0 : z0 + H, 0:R, :] = fill((H, R, C), F32)
            frac[X - 1 if s == 0 else HI, 0:R, :] = jnp.zeros((R, C), F32)
            edge_z[s] = jnp.zeros((2, R, C), F32)

        for t in (0, 1):

            @pl.when(jnp.logical_not(has["x", s] & has["z", t]))
            def _():
                c = 2 * s + t
                corner_in[c] = jnp.zeros((12, 8, C), F32)
                corner_in[c, 4:8, 0:4] = jnp.ones((4, 4, C), F32)

    for n in (4, 5, 6):
        loads[n].wait()
    for s, base in ((0, R - H), (1, 0)):
        for n, a in enumerate(PACKED):
            for i in range(H):
                raw_out[s, 4 * n + i] = ext[a, 0:L, base + i, :]

    pl.semaphore_wait(
        barrier,
        count_z * (1 + has["x", 0].astype(jnp.int32) + has["x", 1].astype(jnp.int32)) - 1,
    )

    def remote(src, dst, sem, device):
        return pltpu.make_async_remote_copy(
            src_ref=src,
            dst_ref=dst,
            send_sem=send_sem.at[sem],
            recv_sem=recv_sem.at[sem],
            device_id=device,
            device_id_type=MESH,
        )

    early, late = [], []
    for s in (0, 1):
        to_x = (gx + 1, gz) if s == 0 else (gx - 1, gz)
        to_z = (gx, gz + 1) if s == 0 else (gx, gz - 1)
        out_x, out_z = has["x", 1 - s], has["z", 1 - s]
        src_l = pl.ds(L - H if s == 0 else 0, H)
        dst_l = pl.ds(LO if s == 0 else HI, H)
        b = 12 * s
        early += [
            (out_x, has["x", s], remote(pc_in, pc.at[1 + s], b + 0, to_x)),
            (out_x, has["x", s], remote(pi_in, pi.at[1 + s], b + 1, to_x)),
            (out_x, has["x", s], remote(raw_out.at[s], raw_in.at[s], b + 2, to_x)),
            (out_z, has["z", s], remote(p_in.at[src_l], ext.at[AP, dst_l, own], b + 3, to_z)),
            (out_z, has["z", s], remote(sto_in.at[src_l], ext.at[AST, dst_l, own], b + 4, to_z)),
            (
                out_z,
                has["z", s],
                remote(tr_in.at[:, src_l], ext.at[pl.ds(AT0, 3), dst_l, own], b + 5, to_z),
            ),
        ]
        late += [
            (out_x, has["x", s], remote(cmp_out.at[s, pl.ds(0, 5)], cmp_in.at[s], b + 6, to_x)),
            (out_x, has["x", s], remote(cmp_out.at[s, pl.ds(5, 2)], edge_x.at[s], b + 7, to_x)),
            (
                out_z,
                has["z", s],
                remote(ext.at[ATO, src_l, own], ext.at[ATO, dst_l, own], b + 8, to_z),
            ),
            (
                out_z,
                has["z", s],
                remote(
                    frac.at[pl.ds(L - 1 if s == 0 else 0, 1), own],
                    frac.at[pl.ds(X - 1 if s == 0 else HI, 1), own],
                    b + 9,
                    to_z,
                ),
            ),
            (out_z, has["z", s], remote(edge_out.at[s], edge_z.at[s], b + 10, to_z)),
        ]
        for t in (0, 1):
            c = 2 * s + t
            to = (to_x[0], gz + 1 if t == 0 else gz - 1)
            late.append(
                (
                    out_x & has["z", 1 - t],
                    has["x", s] & has["z", t],
                    remote(corner_out.at[c], corner_in.at[c], 24 + c, to),
                )
            )

    def start(copies):
        for out, _, copy in copies:

            @pl.when(out)
            def _():
                copy.start()

    start(early)

    for n in (7, 8):
        loads[n].wait()
    for l in range(L):
        total, fraction = mobility(local[0, l], local[1, l])
        ext[ATO, l, 0:R, :] = total
        frac[l, 0:R, :] = fraction

    for s, base in ((0, R - H), (1, 0)):
        for i in range(H):
            cmp_out[s, i] = ext[ATO, 0:L, base + i, :]
        cmp_out[s, 4] = frac[0:L, R - 1 if s == 0 else 0, :]
        inner, outer = (R - H, R - H - 1) if s == 0 else (H - 1, H)
        face = R - H - 1 if s == 0 else H - 1
        rate = (
            ext[AT1, 0:L, face, :]
            * 0.5
            * (ext[ATO, 0:L, inner, :] + ext[ATO, 0:L, outer, :])
        )
        cmp_out[s, 5] = rate
        cmp_out[s, 6] = rate * ext[AP, 0:L, outer, :]
        rate = ext[AT0, face, 0:R, :] * 0.5 * (ext[ATO, inner, 0:R, :] + ext[ATO, outer, 0:R, :])
        edge_out[s, 0] = rate
        edge_out[s, 1] = rate * ext[AP, outer, 0:R, :]
        for t in (0, 1):
            l0 = L - H if t == 0 else 0
            for n, pair in enumerate(PAIRS):
                for i in range(H):
                    for h, a in enumerate(pair):
                        corner_out[2 * s + t, 4 * n + i, 4 * h : 4 * h + 4, :] = ext[
                            a, l0 : l0 + H, base + i, :
                        ]
    start(late)

    for n in (0, 1, 2, 3):
        loads[n].wait()
    cell = lane_groups(pc[0])
    index = lane_groups(pi[0])
    column = [cell_parts(v, gz)[2] for v in cell]
    rows = [one_hot(X * R, own_rows(v, gz)) for v in cell]
    for g in range(GROUPS):
        own_hot[:, 128 * g : 128 * g + 128] = rows[g].astype(BF16)
        cols[0, g : g + 1] = column[g]
        idxs[0, g : g + 1] = index[g]
    hot = jnp.concatenate([one_hot(C, c).astype(BF16) for c in column], axis=1)
    field = ext[ATO, 0:L, 0:R, :].reshape(L * R, C)
    sums = []
    for values in (field * ext[AP, 0:L, 0:R, :].reshape(L * R, C), field):
        high, low = split(values)
        picked = jnp.dot(high, hot, preferred_element_type=F32) + jnp.dot(
            low, hot, preferred_element_type=F32
        )
        part = jnp.zeros((1, 128), F32)
        for g in range(GROUPS):
            chosen = picked[:, 128 * g : 128 * g + 128] * rows[g][0 : L * R]
            part = part + index[g] * jnp.sum(chosen, axis=0, keepdims=True)
        part = part + pltpu.roll(part, 64, 1)
        sums.append(part + pltpu.roll(part, 32, 1))
    aim = four(tgt[...])
    mode = four(ctl[...].astype(F32))
    tile_out[0:1] = sums[0]
    tile_out[1:2] = sums[1]
    tile_out[2:3] = aim
    tile_out[3:4] = mode
    tile_out[4:8] = jnp.zeros((4, 128), F32)
    tiles[4 + gz] = tile_out[...]

    def tile_copy(dx, dz, z):
        slot = 4 * (1 - dx) + z
        sem = 28 + 7 * (dx + 1) + dz + 3
        return pltpu.make_async_remote_copy(
            src_ref=tile_out,
            dst_ref=tiles.at[slot],
            send_sem=send_sem.at[sem],
            recv_sem=recv_sem.at[sem],
            device_id=(gx + dx, gz + dz),
            device_id_type=MESH,
        )

    ties = []
    for dx in (-1, 0, 1):
        for dz in range(-3, 4):
            if dx == 0 and dz == 0:
                continue
            out = (gz + dz >= 0) & (gz + dz < count_z)
            came = (gz - dz >= 0) & (gz - dz < count_z)
            if dx:
                out = out & has["x", 1 if dx > 0 else 0]
                came = came & has["x", 0 if dx > 0 else 1]
            ties.append((out, came, dx, dz))
    for out, _, dx, dz in ties:

        @pl.when(out)
        def _():
            tile_copy(dx, dz, gz).start()

    index_sum[:, 0:R, :] = scatter(own_hot[...], column_values(column, index)).reshape(X, R, C)
    for s in (0, 1):
        for _, came, copy in early[6 * s : 6 * s + 2]:

            @pl.when(came)
            def _():
                copy.wait_recv()

        cell = lane_groups(pc[1 + s])
        index = lane_groups(pi[1 + s])
        for g in range(GROUPS):
            side_hot[:, 512 * s + 128 * g : 512 * s + 128 * g + 128] = one_hot(
                X * 8, side_rows(cell[g], gz, s)
            ).astype(BF16)
            cols[1 + s, g : g + 1] = cell_parts(cell[g], gz)[2]
            idxs[1 + s, g : g + 1] = index[g]
        part = scatter(
            side_hot[:, 512 * s : 512 * s + 512],
            column_values([cell_parts(v, gz)[2] for v in cell], index),
        ).reshape(X, 8, C)
        if s == 0:
            index_sum[:, R:X, :] = part
        else:
            index_sum[:, R:X, :] += part

    for n, (_, came, copy) in enumerate(early):
        if n % 6 < 2:
            continue

        @pl.when(came)
        def _():
            copy.wait_recv()

    for s, base in ((0, LO), (1, HI)):
        for n, a in enumerate(PACKED):
            for i in range(H):
                ext[a, 0:L, base + i, :] = raw_in[s, 4 * n + i]
    for _, came, copy in late:

        @pl.when(came)
        def _():
            copy.wait_recv()

    for s, base in ((0, LO), (1, HI)):
        for i in range(H):
            ext[ATO, 0:L, base + i, :] = cmp_in[s, i]
        frac[0:L, X - 1 if s == 0 else HI, :] = cmp_in[s, 4]
        for t in (0, 1):
            l0 = LO if t == 0 else HI
            for n, pair in enumerate(PAIRS):
                for i in range(H):
                    for h, a in enumerate(pair):
                        ext[a, l0 : l0 + H, base + i, :] = corner_in[
                            2 * s + t, 4 * n + i, 4 * h : 4 * h + 4, :
                        ]

    for out, came, dx, dz in ties:

        @pl.when(came)
        def _():
            tile_copy(dx, dz, gz - dz).wait_recv()

    for out, _, copy in early + late:

        @pl.when(out)
        def _():
            copy.wait_send()

    for out, _, dx, dz in ties:

        @pl.when(out)
        def _():
            tile_copy(dx, dz, gz).wait_send()

    loads[9].wait()


def shift_rows(value, by):
    return pltpu.roll(value, by % value.shape[0], 0)


def shift_columns(value, by):
    return pltpu.roll(value, by % C, 1)


def solve(
    count_x,
    count_z,
    ext,
    frac,
    local,
    index_sum,
    own_hot,
    side_hot,
    cols,
    idxs,
    edge_x,
    edge_z,
    tiles,
    new_p,
    residual,
    new_s,
    new_h,
    hole,
    coef,
    face,
    source,
    field,
    out_p,
    out_r,
    out_s,
    out_h,
    sems,
):
    gx, gz = lax.axis_index("gx"), lax.axis_index("gz")

    holes = []
    for d in range(3):
        tile = tiles[4 * d] + tiles[4 * d + 1] + tiles[4 * d + 2] + tiles[4 * d + 3]
        sum_p, sum_w = tile[0:1], tile[1:2]
        aim, mode = tiles[4 * d][2:3], tiles[4 * d][3:4]
        holes.append(jnp.where(mode == 0.0, (aim + sum_p) / sum_w, aim))
    hole[...] = holes[1][:, 0:WELLS]

    def spread(n, bottom):
        return column_values(
            [cols[n, g : g + 1] for g in range(GROUPS)],
            [idxs[n, g : g + 1] * bottom for g in range(GROUPS)],
        )

    source[:, 0:R, :] = scatter(own_hot[...], spread(0, holes[1])).reshape(X, R, C)
    source[:, R:X, :] = scatter(
        side_hot[...], jnp.concatenate([spread(1, holes[0]), spread(2, holes[2])], axis=1)
    ).reshape(X, 8, C)

    row = lax.broadcasted_iota(jnp.int32, (X, C), 0)
    column = lax.broadcasted_iota(jnp.int32, (X, C), 1)
    cut_row = (row == LO - 1) | ((row == R - 1) & (gx == count_x - 1))
    row_half = jnp.where(cut_row, 0.0, 0.5)
    column_half = jnp.where(column == C - 1, 0.0, 0.5)
    layer_half = jnp.where(gz == count_z - 1, 0.0, 0.5)
    tail = lax.broadcasted_iota(jnp.int32, (8, C), 0)

    def layer_face(l):
        if l == LO - 1:
            return jnp.zeros((X, C), F32)
        half = layer_half if l == L - 1 else 0.5
        return ext[AT0, l] * half * (ext[ATO, l] + ext[ATO, (l + 1) % X])

    below = layer_face(X - 1)
    for l in range(X):
        total, p, storage = ext[ATO, l], ext[AP, l], ext[AST, l]
        above = layer_face(l)
        next_row = ext[AT1, l] * row_half * (total + shift_rows(total, -1))
        prev_row = shift_rows(next_row, 1)
        next_col = ext[AT2, l] * column_half * (total + shift_columns(total, -1))
        prev_col = shift_columns(next_col, 1)
        src = total * (source[l] - p * index_sum[l])
        diag = storage + above + below + next_row + prev_row + next_col + prev_col
        rhs = storage * p + src
        if l < L:
            source[l] = src
            low, high = edge_x[0, :, l : l + 1, :], edge_x[1, :, l : l + 1, :]
            pick = [
                jnp.where(tail == 3, high[n], jnp.where(tail == 4, low[n], 0.0)) for n in (0, 1)
            ]
            pad = jnp.zeros((R, C), F32)
            diag = diag + jnp.concatenate([pad, pick[0]], axis=0)
            rhs = rhs + jnp.concatenate([pad, pick[1]], axis=0)
        elif l in (LO - 1, LO):
            side = edge_z[1 if l == LO - 1 else 0]
            pad = jnp.zeros((X - R, C), F32)
            diag = diag + jnp.concatenate([side[0], pad], axis=0)
            rhs = rhs + jnp.concatenate([side[1], pad], axis=0)
        inverse = 1.0 / diag
        for n, value in enumerate((rhs, above, below, next_row, prev_row, next_col, prev_col)):
            coef[n, l] = value * inverse
        if l < L or l == X - 1:
            face[0, l] = above
            face[1, l] = next_row
            face[2, l] = next_col
        below = above

    for sweep in range(4):
        layers = [l % X for l in range(-(3 - sweep) - 1, L + 4 - sweep)]
        for l in layers:
            if sweep == 0:
                p, up, down = ext[AP, l], ext[AP, (l + 1) % X], ext[AP, (l - 1) % X]
            else:
                old = (sweep - 1) % 2
                p, up, down = field[old, l], field[old, (l + 1) % X], field[old, (l - 1) % X]
            field[sweep % 2, l] = (
                coef[0, l]
                + coef[1, l] * up
                + coef[2, l] * down
                + coef[3, l] * shift_rows(p, -1)
                + coef[4, l] * shift_rows(p, 1)
                + coef[5, l] * shift_columns(p, -1)
                + coef[6, l] * shift_columns(p, 1)
            )

    writes = []
    final = 1

    def layer_flow(l):
        k, n = l % X, (l + 1) % X
        flow = face[0, k, 0:R, :] * (field[final, k, 0:R, :] - field[final, n, 0:R, :])
        return flow, flow * jnp.where(flow > 0, frac[k, 0:R, :], frac[n, 0:R, :])

    below, gas_below = layer_flow(-1)
    for l in range(L):
        p, part = field[final, l], frac[l]
        above, gas_above = layer_flow(l)
        flow = face[1, l] * (p - shift_rows(p, -1))
        gas = flow * jnp.where(flow > 0, part, shift_rows(part, -1))
        net = (flow - shift_rows(flow, 1))[0:R] + above - below
        out = (gas - shift_rows(gas, 1))[0:R] + gas_above - gas_below
        p, part = p[0:R], part[0:R]
        flow = face[2, l, 0:R, :] * (p - shift_columns(p, -1))
        gas = flow * jnp.where(flow > 0, part, shift_columns(part, -1))
        net = net + flow - shift_columns(flow, 1)
        out = out + gas - shift_columns(gas, 1)
        src = source[l, 0:R, :]
        out_p[l] = p
        out_r[l] = ext[AST, l, 0:R, :] * (ext[AP, l, 0:R, :] - p) + src - net
        gas_source = jnp.maximum(src, 0.0) + jnp.minimum(src, 0.0) * part
        saturation = local[0, l] + local[2, l] * (gas_source - out)
        out_s[l] = saturation
        out_h[l] = jnp.maximum(local[1, l], saturation)
        below, gas_below = above, gas_above
    for n, (src, dst) in enumerate(
        ((out_p, new_p), (out_r, residual), (out_s, new_s), (out_h, new_h))
    ):
        copy = pltpu.make_async_copy(src, dst, sems.at[n])
        copy.start()
        writes.append(copy)
    for copy in writes:
        copy.wait()


def body(
    count_x,
    count_z,
    pressure,
    saturation,
    sat_history,
    storage,
    step_volume,
    transmiss,
    perf_cell,
    perf_index,
    control,
    target,
):
    vmem = pl.BlockSpec(memory_space=pltpu.VMEM)
    hbm = pl.BlockSpec(memory_space=pltpu.HBM)
    dma = pltpu.SemaphoreType.DMA
    block = (L, R, C)
    mid = pl.pallas_call(
        functools.partial(exchange, count_x, count_z),
        out_shape=(
            pltpu.VMEM((6, X, X, C), F32),
            pltpu.VMEM((X, X, C), F32),
            pltpu.VMEM((3, *block), F32),
            pltpu.VMEM((X, X, C), F32),
            pltpu.VMEM((X * R, 512), BF16),
            pltpu.VMEM((X * 8, 1024), BF16),
            pltpu.VMEM((3, 8, 128), jnp.int32),
            pltpu.VMEM((3, 8, 128), F32),
            pltpu.VMEM((2, 2, L, C), F32),
            pltpu.VMEM((2, 2, R, C), F32),
            pltpu.VMEM((12, 8, 128), F32),
        ),
        in_specs=[hbm] * 10,
        out_specs=[vmem] * 11,
        scratch_shapes=[
            pltpu.VMEM((2, RAW, L, C), F32),
            pltpu.VMEM((2, RAW, L, C), F32),
            pltpu.VMEM((2, 7, L, C), F32),
            pltpu.VMEM((2, 5, L, C), F32),
            pltpu.VMEM((4, 12, 8, C), F32),
            pltpu.VMEM((4, 12, 8, C), F32),
            pltpu.VMEM((2, 2, R, C), F32),
            pltpu.VMEM((8, 128), F32),
            pltpu.VMEM((3, NP, WELLS), jnp.int32),
            pltpu.VMEM((3, NP, WELLS), F32),
            pltpu.VMEM((1, WELLS), jnp.int32),
            pltpu.VMEM((1, WELLS), F32),
            dma((10,)),
            dma((49,)),
            dma((49,)),
        ],
        compiler_params=pltpu.CompilerParams(
            collective_id=0, has_side_effects=True, vmem_limit_bytes=VMEM_LIMIT
        ),
        name="exchange",
    )(
        pressure,
        saturation,
        sat_history,
        storage,
        step_volume,
        transmiss,
        perf_cell.T,
        perf_index.T,
        control.reshape(1, WELLS),
        target.reshape(1, WELLS),
    )
    whole = jax.ShapeDtypeStruct(block, F32)
    *fields, hole = pl.pallas_call(
        functools.partial(solve, count_x, count_z),
        out_shape=(whole, whole, whole, whole, jax.ShapeDtypeStruct((1, WELLS), F32)),
        in_specs=[vmem] * 11,
        out_specs=[hbm] * 4 + [vmem],
        scratch_shapes=[
            pltpu.VMEM((7, X, X, C), F32),
            pltpu.VMEM((3, X, X, C), F32),
            pltpu.VMEM((X, X, C), F32),
            pltpu.VMEM((2, X, X, C), F32),
            pltpu.VMEM(block, F32),
            pltpu.VMEM(block, F32),
            pltpu.VMEM(block, F32),
            pltpu.VMEM(block, F32),
            dma((4,)),
        ],
        compiler_params=pltpu.CompilerParams(vmem_limit_bytes=VMEM_LIMIT),
        name="solve",
    )(*mid)
    return (*fields, hole.reshape(WELLS))


def solution(mesh):
    cells = P("gz", "gx", None)
    return jax.shard_map(
        functools.partial(body, mesh.shape["gx"], mesh.shape["gz"]),
        mesh=mesh,
        in_specs=(
            *[cells] * 5,
            P(None, "gz", "gx", None),
            P("gx", None),
            P("gx", None),
            P("gx"),
            P("gx"),
        ),
        out_specs=(*[cells] * 4, P("gx")),
        check_vma=False,
    )
```

time: 144 us -> 48.2 us (0.33)
  the two profiles are of different devices: /device:TPU:26 before, /device:TPU:24 now
where the time goes in v1:
time: 48.2 us; the launch traced here: 47.5 us
  Pallas kernels  38.2 us (79%)
  local copies, waits for them, and re-layouts  8.58 us (18%)
  between operations  0.66 us (1%)
    pallas_call x1, Pallas kernels, body(): pl.pallas_call(functools.partial(exchange, count_x, count_z), out_shape=(...  32.4 us
    unnamed x20, local copies, waits for them, and re-layouts  8.58 us
    pallas_call x1, Pallas kernels, body(): pl.pallas_call(functools.partial(solve, count_x, count_z), out_shape=(who...  5.8 us

profile of v1, /device:TPU:24, one launch (start us, length us, event | category | flops | bytes accessed | tf_op | source)
XLA Modules:
  0.0 47.5 jit_solution(8076306972430227898)
XLA Ops:
  0.6 0.0 copy-start
  0.6 1.1 %copy-done = f32[3,16,16,256]{3,2,1,0:T(8,128)S(1)} copy-done((f32[3,16,16,256]{3,2,1,0:T(8,128)S(1)}, f32[3,16,16,256]{3,2,1,0:T(8,128)}, u32[]{:S(2)}) %copy-start) | copy-done | bytes 786456
  1.8 0.0 copy-start.1
  1.8 0.9 %copy-done.1 = f32[16,16,256]{2,1,0:T(8,128)S(1)} copy-done((f32[16,16,256]{2,1,0:T(8,128)S(1)}, f32[16,16,256]{2,1,0:T(8,128)}, u32[]{:S(2)}) %copy-start.1) | copy-done | bytes 262168
  2.7 0.0 copy-start.2
  2.7 0.9 %copy-done.2 = f32[16,16,256]{2,1,0:T(8,128)S(1)} copy-done((f32[16,16,256]{2,1,0:T(8,128)S(1)}, f32[16,16,256]{2,1,0:T(8,128)}, u32[]{:S(2)}) %copy-start.2) | copy-done | bytes 262168
  3.7 0.0 copy-start.3
  3.7 0.9 %copy-done.3 = f32[16,16,256]{2,1,0:T(8,128)S(1)} copy-done((f32[16,16,256]{2,1,0:T(8,128)S(1)}, f32[16,16,256]{2,1,0:T(8,128)}, u32[]{:S(2)}) %copy-start.3) | copy-done | bytes 262168
  4.6 0.0 copy-start.4
  4.6 0.9 %copy-done.4 = f32[16,16,256]{2,1,0:T(8,128)S(1)} copy-done((f32[16,16,256]{2,1,0:T(8,128)S(1)}, f32[16,16,256]{2,1,0:T(8,128)}, u32[]{:S(2)}) %copy-start.4) | copy-done | bytes 262168
  5.6 0.0 copy-start.5
  5.6 0.9 %copy-done.5 = f32[16,16,256]{2,1,0:T(8,128)S(1)} copy-done((f32[16,16,256]{2,1,0:T(8,128)S(1)}, f32[16,16,256]{2,1,0:T(8,128)}, u32[]{:S(2)}) %copy-start.5) | copy-done | bytes 262168
  6.5 0.0 copy-start.6
  6.5 0.7 %copy-done.6 = s32[32,16]{0,1:T(8,128)S(1)} copy-done((s32[32,16]{0,1:T(8,128)S(1)}, s32[32,16]{0,1:T(8,128)}, u32[]{:S(2)}) %copy-start.6) | copy-done | bytes 2072
  7.2 0.0 copy-start.7
  7.2 0.7 %copy-done.7 = f32[32,16]{0,1:T(8,128)S(1)} copy-done((f32[32,16]{0,1:T(8,128)S(1)}, f32[32,16]{0,1:T(8,128)}, u32[]{:S(2)}) %copy-start.7) | copy-done | bytes 2072
  7.9 0.0 copy-start.8
  7.9 0.7 %copy-done.8 = s32[32]{0:T(128)S(1)} copy-done((s32[32]{0:T(128)S(1)}, s32[32]{0:T(128)}, u32[]{:S(2)}) %copy-start.8) | copy-done | bytes 152
  8.6 0.0 copy-start.9
  8.6 0.7 %copy-done.9 = f32[32]{0:T(128)S(1)} copy-done((f32[32]{0:T(128)S(1)}, f32[32]{0:T(128)}, u32[]{:S(2)}) %copy-start.9) | copy-done | bytes 152
  9.2 32.4 %exchange.1 = (f32[6,24,24,256]{3,2,1,0:T(8,128)S(1)}, f32[24,24,256]{2,1,0:T(8,128)S(1)}, f32[3,16,16,256]{3,2,1,0:T(8,128)S(1)}, f32[24,24,256]{2,1,0:T(8,128)...) custom-call(f32[16,16,256]{2,1,0:T(8,128)S(1)} %copy-done.1, ...), custom_call_target="tpu_custom_call" | custom-call | tf_op jit(solution)/shard_map/exchange/pallas_call | solution.py:659
  41.7 5.8 %solve.1 = (f32[16,16,256]{2,1,0:T(8,128)}, f32[16,16,256]{2,1,0:T(8,128)}, f32[16,16,256]{2,1,0:T(8,128)}, f32[16,16,256]{2,1,0:T(8,128)}, f32[1,32]{1,0:T(1,128)}) custom-call(f32[6,24,24,256]{3,2,1,0:T(8,128)S(1)} %get-tuple-element.21.ext, f32[24,24,256]{2,1,0:T(8,128)S(1)} %get-tuple-element.22.frac, f32[3,16,16,256]{3,2,1,0:T(8,128)S(1)} %get-tuple-element.23.local, ...), custom_call_target="tpu_custom_call" | custom-call | tf_op jit(solution)/shard_map/solve/pallas_call | solution.py:710
Async XLA Ops:
  0.6 1.1 %copy-start = (f32[3,16,16,256]{3,2,1,0:T(8,128)S(1)}, f32[3,16,16,256]{3,2,1,0:T(8,128)}, u32[]{:S(2)}) copy-start(f32[3,16,16,256]{3,2,1,0:T(8,128)} %tr_in.1) | copy-start | bytes 2359300
  1.8 0.9 %copy-start.1 = (f32[16,16,256]{2,1,0:T(8,128)S(1)}, f32[16,16,256]{2,1,0:T(8,128)}, u32[]{:S(2)}) copy-start(f32[16,16,256]{2,1,0:T(8,128)} %p_in.1) | copy-start | bytes 786436
  2.7 0.9 %copy-start.2 = (f32[16,16,256]{2,1,0:T(8,128)S(1)}, f32[16,16,256]{2,1,0:T(8,128)}, u32[]{:S(2)}) copy-start(f32[16,16,256]{2,1,0:T(8,128)} %sat_in.1) | copy-start | bytes 786436
  3.7 0.9 %copy-start.3 = (f32[16,16,256]{2,1,0:T(8,128)S(1)}, f32[16,16,256]{2,1,0:T(8,128)}, u32[]{:S(2)}) copy-start(f32[16,16,256]{2,1,0:T(8,128)} %hist_in.1) | copy-start | bytes 786436
  4.6 0.9 %copy-start.4 = (f32[16,16,256]{2,1,0:T(8,128)S(1)}, f32[16,16,256]{2,1,0:T(8,128)}, u32[]{:S(2)}) copy-start(f32[16,16,256]{2,1,0:T(8,128)} %sto_in.1) | copy-start | bytes 786436
  5.6 0.9 %copy-start.5 = (f32[16,16,256]{2,1,0:T(8,128)S(1)}, f32[16,16,256]{2,1,0:T(8,128)}, u32[]{:S(2)}) copy-start(f32[16,16,256]{2,1,0:T(8,128)} %vol_in.1) | copy-start | bytes 786436
  6.5 0.7 %copy-start.6 = (s32[32,16]{0,1:T(8,128)S(1)}, s32[32,16]{0,1:T(8,128)}, u32[]{:S(2)}) copy-start(s32[32,16]{0,1:T(8,128)} %param.16) | copy-start | bytes 6148
  7.2 0.7 %copy-start.7 = (f32[32,16]{0,1:T(8,128)S(1)}, f32[32,16]{0,1:T(8,128)}, u32[]{:S(2)}) copy-start(f32[32,16]{0,1:T(8,128)} %param.17) | copy-start | bytes 6148
  7.9 0.7 %copy-start.8 = (s32[32]{0:T(128)S(1)}, s32[32]{0:T(128)}, u32[]{:S(2)}) copy-start(s32[32]{0:T(128)} %param.18) | copy-start | bytes 388
  8.6 0.7 %copy-start.9 = (f32[32]{0:T(128)S(1)}, f32[32]{0:T(128)}, u32[]{:S(2)}) copy-start(f32[32]{0:T(128)} %param.19) | copy-start | bytes 388

commit v2 on v0

v2 whole, which is shorter than its diff:
```python
import functools

import jax
import jax.numpy as jnp
from jax import lax
from jax.experimental import pallas as pl
from jax.experimental.pallas import tpu as pltpu
from jax.sharding import PartitionSpec as P

L = 16
R = 16
C = 256
WELLS = 32
NP = 16
GROUPS = WELLS * NP // 128
SIDES = range(4)
MESH = pl.DeviceIdType.MESH
F32 = jnp.float32
BF16 = jnp.bfloat16
VMEM_LIMIT = 26 * 2**20


def mobility(sat, history):
    trapped = history / (1.0 + 1.5 * history)
    excess = jnp.maximum(sat - trapped, 0.0)
    free_gas = 0.5 * (excess + jnp.sqrt(excess * excess + excess / 0.375))
    relperm = jnp.where(sat < history, free_gas * free_gas, sat * sat)
    gas = relperm / 0.5
    total = (1.0 - sat) * (1.0 - sat) + gas
    return (total, gas / total)


def split(values):
    high = values.astype(BF16)
    low = (values - high.astype(F32)).astype(BF16)
    return high, low


def four(row):
    return jnp.concatenate([row, row, row, row], axis=1)


def lane_groups(table):
    wide = four(table)
    place = lax.broadcasted_iota(jnp.int32, (1, 128), 1) // WELLS
    rows = []
    for g in range(GROUPS):
        row = wide[4 * g : 4 * g + 1]
        for k in range(1, 4):
            row = jnp.where(place == k, wide[4 * g + k : 4 * g + k + 1], row)
        rows.append(row)
    return rows


def cell_parts(cell, gz):
    layer = lax.shift_right_logical(cell, 12) - gz * L
    return layer, lax.shift_right_logical(cell, 8) & (R - 1), cell & (C - 1)


def one_hot(size, target):
    return jnp.where(lax.broadcasted_iota(jnp.int32, (size, 128), 0) == target, 1.0, 0.0)


def own_rows(cell, gz):
    layer, row, _ = cell_parts(cell, gz)
    index = jnp.where(layer == -1, L + 1, layer)
    return jnp.where((layer >= -1) & (layer <= L), index * R + row, -1)


def side_rows(cell, gz, side):
    layer, row, _ = cell_parts(cell, gz)
    return jnp.where((layer >= 0) & (layer < L) & (row == (0 if side else R - 1)), layer, -1)


def column_values(columns, values):
    place = lax.broadcasted_iota(jnp.int32, (C, 128), 0)
    return jnp.concatenate(
        [jnp.where(place == c, v, 0.0) for c, v in zip(columns, values)], axis=1
    )


def shift_rows(value, by):
    return pltpu.roll(value, by % value.shape[0], 0)


def shift_columns(value, by):
    return pltpu.roll(value, by % C, 1)


def near_end(side):
    return 15 * (side % 2)


def plane(ref, side, k):
    return ref[0:L, k, :] if side < 2 else ref[k, 0:R, :]


def add_to_plane(ref, side, k, value):
    if side < 2:
        ref[0:L, k, :] += value
    else:
        ref[k, 0:R, :] += value


def ends(side):
    for e in (0, 1):
        yield e, 15 * e, 2 * side + e if side < 2 else 2 * e + side - 2


def planes(ref, side, n):
    return ref[side, 16 * n : 16 * n + 16]


def inner_sum(start, p, up, down, above, below, next_row, next_col):
    value = start + next_row * shift_rows(p, -1) + shift_rows(next_row * p, 1)
    value = value + next_col * shift_columns(p, -1) + shift_columns(next_col * p, 1)
    if up is not None:
        value = value + above * up
    if down is not None:
        value = value + below * down
    return value


def sweep_layer(ref, rhs, face, l):
    return inner_sum(
        rhs[l],
        ref[l],
        ref[l + 1] if l < L - 1 else None,
        ref[l - 1] if l else None,
        face[0, l],
        face[0, l - 1] if l else None,
        face[1, l],
        face[2, l],
    )


def exchange(
    count_x,
    count_z,
    p_in,
    sat_in,
    hist_in,
    sto_in,
    vol_in,
    tr_in,
    pc_in,
    pi_in,
    ctl_in,
    tgt_in,
    storage,
    local,
    frac,
    face,
    inverse,
    rhs,
    source,
    second,
    third,
    border,
    weight,
    over_ring,
    end_face,
    over_corner,
    bulk_in,
    mid_in,
    last_in,
    last_corner_in,
    hole,
    p0,
    total,
    trans,
    num,
    diag,
    first,
    ring,
    index_sum,
    side_index,
    own_source,
    side_source,
    own_hot,
    side_hot,
    column_hot,
    spread,
    near_out,
    near_in,
    corner_out,
    corner_in,
    bulk_out,
    mid_out,
    last_out,
    last_corner_out,
    perf_out,
    perf_in,
    tile_out,
    tiles,
    pc,
    pi,
    ctl,
    tgt,
    send_sem,
    recv_sem,
):
    gx, gz = lax.axis_index("gx"), lax.axis_index("gz")
    has = (gx > 0, gx < count_x - 1, gz > 0, gz < count_z - 1)

    barrier = pltpu.get_barrier_semaphore()

    def signal_column(x):
        def one(z, carry):
            pl.semaphore_signal(barrier, inc=1, device_id=(x, z), device_id_type=MESH)
            return carry

        return one

    def others(z, carry):
        @pl.when(z != gz)
        def _():
            pl.semaphore_signal(barrier, inc=1, device_id=(gx, z), device_id_type=MESH)

        return carry

    for s in (0, 1):

        @pl.when(has[s])
        def _():
            lax.fori_loop(0, count_z, signal_column(gx + 2 * s - 1), 0)

    lax.fori_loop(0, count_z, others, 0)

    loads = [
        pltpu.make_async_copy(pc_in, pc, send_sem.at[0]),
        pltpu.make_async_copy(pi_in, pi, send_sem.at[1]),
        pltpu.make_async_copy(sat_in, local.at[0], send_sem.at[2]),
        pltpu.make_async_copy(hist_in, local.at[1], send_sem.at[3]),
        pltpu.make_async_copy(p_in, p0, send_sem.at[4]),
        pltpu.make_async_copy(ctl_in, ctl, send_sem.at[5]),
        pltpu.make_async_copy(tgt_in, tgt, send_sem.at[6]),
        pltpu.make_async_copy(tr_in, trans, send_sem.at[7]),
        pltpu.make_async_copy(sto_in, storage, send_sem.at[8]),
        pltpu.make_async_copy(vol_in, local.at[2], send_sem.at[9]),
    ]
    for copy in loads:
        copy.start()

    for side in SIDES:

        @pl.when(jnp.logical_not(has[side]))
        def _():
            near_in[side] = jnp.zeros((88, C), F32)
            near_in[side, 48:64] = jnp.ones((16, C), F32)
            bulk_in[side] = jnp.zeros((64, C), F32)
            mid_in[side] = jnp.zeros((24, C), F32)
            last_in[side] = jnp.zeros((48, C), F32)
            if side < 2:
                perf_in[side] = jnp.where(
                    lax.broadcasted_iota(jnp.int32, (NP, 128), 1) < WELLS, 1e9, 0.0
                )
                tiles[8 * side : 8 * side + 4] = jnp.ones((4, 1, 128), F32)

    for c in range(4):

        @pl.when(jnp.logical_not(has[c // 2] & has[2 + c % 2]))
        def _():
            corner_in[c] = jnp.zeros((8, C), F32)
            corner_in[c, 4:5] = jnp.ones((1, C), F32)
            last_corner_in[c] = jnp.zeros((4, C), F32)

    for n in (0, 1):
        loads[n].wait()
    cell = lane_groups(pc[...])
    own_index = lane_groups(pi[...])
    own_column = [cell_parts(v, gz)[2] for v in cell]
    own_row = [own_rows(v, gz) for v in cell]
    for g in range(GROUPS):
        part = slice(128 * g, 128 * g + 128)
        own_hot[:, part] = one_hot((L + 2) * R, own_row[g]).astype(BF16)
        column_hot[:, part] = one_hot(C, own_column[g]).astype(BF16)
    table = jnp.concatenate([pc[...].astype(F32), pi[...]], axis=1)
    perf_out[...] = jnp.concatenate([table, table], axis=1)

    for n in (2, 3):
        loads[n].wait()
    for l in range(L):
        total[l], frac[l] = mobility(local[0, l], local[1, l])
    for n in (4, 7, 8):
        loads[n].wait()

    row = lax.broadcasted_iota(jnp.int32, (R, C), 0)
    column = lax.broadcasted_iota(jnp.int32, (R, C), 1)
    row_half = jnp.where(row == R - 1, 0.0, 0.5)
    column_half = jnp.where(column == C - 1, 0.0, 0.5)
    below = None
    for l in range(L):
        here = total[l]
        next_row = trans[1, l] * row_half * (here + shift_rows(here, -1))
        next_col = trans[2, l] * column_half * (here + shift_columns(here, -1))
        above = trans[0, l] * 0.5 * (here + total[l + 1]) if l < L - 1 else None
        num[l] = inner_sum(
            storage[l] * p0[l],
            p0[l],
            p0[l + 1] if l < L - 1 else None,
            p0[l - 1] if l else None,
            above,
            below,
            next_row,
            next_col,
        )
        bottom = storage[l] + next_row + shift_rows(next_row, 1)
        bottom = bottom + next_col + shift_columns(next_col, 1)
        if l:
            bottom = bottom + below
        if l < L - 1:
            bottom = bottom + above
        diag[l] = bottom
        face[0, l] = above if l < L - 1 else jnp.zeros((R, C), F32)
        face[1, l] = next_row
        face[2, l] = next_col
        below = above

    for side in SIDES:
        k = 15 - near_end(side)
        normal, along = (1, 0) if side < 2 else (0, 1)
        for n, ref in enumerate((p0, total, num, diag, trans.at[normal])):
            near_out[side, 16 * n : 16 * n + 16] = plane(ref, side, k)
        if side < 2:
            near_out[side, 80:81] = trans[along, L - 1, k : k + 1, :]
        else:
            near_out[side, 80:81] = trans[along, k, R - 1 : R, :]
        behind = min(k, 14)
        for n, (ref, at) in enumerate(
            ((face.at[along], k), (face.at[normal], behind), (face.at[2], k), (frac, k))
        ):
            bulk_out[side, 16 * n : 16 * n + 16] = plane(ref, side, at)
    for c in range(4):
        k, m = 15 - 15 * (c // 2), 15 - 15 * (c % 2)
        for n, ref in enumerate((p0, total, trans.at[0], trans.at[1], diag)):
            corner_out[c, n : n + 1] = ref[m, k : k + 1, :]

    for n in (5, 6, 9):
        loads[n].wait()
    field = total[...].reshape(L * R, C)
    parts = split(field * p0[...].reshape(L * R, C)) + split(field)
    picked = jnp.dot(
        jnp.concatenate(parts, axis=0), column_hot[...], preferred_element_type=F32
    )
    place = lax.broadcasted_iota(jnp.int32, (L * R, 128), 0)
    sums = []
    for n in (0, 1):
        part = jnp.zeros((1, 128), F32)
        for g in range(GROUPS):
            pair = picked[2 * n * L * R : 2 * (n + 1) * L * R, 128 * g : 128 * g + 128]
            chosen = jnp.where(place == own_row[g], pair[0 : L * R] + pair[L * R :], 0.0)
            part = part + own_index[g] * jnp.sum(chosen, axis=0, keepdims=True)
        part = part + pltpu.roll(part, 64, 1)
        sums.append(part + pltpu.roll(part, 32, 1))
    quarter = lax.broadcasted_iota(jnp.int32, (1, 128), 1) // WELLS
    packed = jnp.where(quarter == 0, sums[0], sums[1])
    packed = jnp.where(quarter == 2, four(tgt[...]), packed)
    packed = jnp.where(quarter == 3, four(ctl[...].astype(F32)), packed)
    tile_out[...] = packed
    tiles[4 + gz] = packed

    pl.semaphore_wait(
        barrier, count_z * (1 + has[0].astype(jnp.int32) + has[1].astype(jnp.int32)) - 1
    )

    def target(side):
        step = 1 - 2 * (side % 2)
        return (gx + step, gz) if side < 2 else (gx, gz + step)

    def remote(src, dst, send, recv, device):
        return pltpu.make_async_remote_copy(
            src_ref=src,
            dst_ref=dst,
            send_sem=send_sem.at[send],
            recv_sem=recv_sem.at[recv],
            device_id=device,
            device_id_type=MESH,
        )

    near, perf, bulk, mid, last = [], [], [], [], []
    for c in range(4):
        s, t = c // 2, 2 + c % 2
        ok = (has[s ^ 1] & has[t ^ 1], has[s] & has[t])
        to = (target(s)[0], target(t)[1])
        near.append((*ok, remote(corner_out.at[c], corner_in.at[c], 4 + c, 4 + c, to)))
        last.append((*ok, remote(last_corner_out.at[c], last_corner_in.at[c], 4 + c, 18 + c, to)))
    for side in SIDES:
        ok, to = (has[side ^ 1], has[side]), target(side)
        near.append((*ok, remote(near_out.at[side], near_in.at[side], side, side, to)))
        bulk.append((*ok, remote(bulk_out.at[side], bulk_in.at[side], 22 + side, 10 + side, to)))
        mid.append((*ok, remote(mid_out.at[side], mid_in.at[side], side, 34 + side, to)))
        last.append((*ok, remote(last_out.at[side], last_in.at[side], 22 + side, 14 + side, to)))
    for side in (0, 1):
        ok, to = (has[side ^ 1], has[side]), target(side)
        perf.append((*ok, remote(perf_out, perf_in.at[side], 8 + side, 8 + side, to)))

    def start(copies):
        for out, _, copy in copies:

            @pl.when(out)
            def _():
                copy.start()

    def arrive(copies):
        for _, came, copy in copies:

            @pl.when(came)
            def _():
                copy.wait_recv()

    def sent(copies):
        for out, _, copy in copies:

            @pl.when(out)
            def _():
                copy.wait_send()

    def tile_copy(dx, z_from, z_to):
        return pltpu.make_async_remote_copy(
            src_ref=tile_out,
            dst_ref=tiles.at[4 * (1 - dx) + z_from],
            send_sem=send_sem.at[10 + 4 * (1 - dx) + z_to],
            recv_sem=recv_sem.at[22 + 4 * (1 - dx) + z_from],
            device_id=(gx + dx, z_to),
            device_id_type=MESH,
        )

    start(perf)
    ties = []
    for dx in (1, -1, 0):
        for z in range(4):
            if dx:
                ok = (has[1 if dx > 0 else 0], has[0 if dx > 0 else 1])
            else:
                ok = (gz != z, gz != z)
            ties.append((*ok, dx, z))
    for out, _, dx, z in ties:

        @pl.when(out)
        def _():
            tile_copy(dx, gz, z).start()

    start(near)

    start(bulk)

    def place_index(d, columns, indices):
        high, low = split(column_values(columns, indices).T)
        spread[0, 512 * d : 512 * d + 512, :] = high
        spread[1, 512 * d : 512 * d + 512, :] = low

    def product(rows, n, d):
        return jnp.dot(
            rows, spread[n, 512 * d : 512 * d + 512, :], preferred_element_type=F32
        )

    place_index(2, own_column, own_index)
    index_sum[...] = (product(own_hot[...], 0, 2) + product(own_hot[...], 1, 2)).reshape(
        L + 2, R, C
    )
    arrive(perf)
    for side in (0, 1):
        table = perf_in[side]
        cell = lane_groups(table[:, 0:WELLS].astype(jnp.int32))
        for g in range(GROUPS):
            side_hot[side, :, 128 * g : 128 * g + 128] = one_hot(
                L, side_rows(cell[g], gz, side)
            ).astype(BF16)
        place_index(
            side,
            [cell_parts(v, gz)[2] for v in cell],
            lane_groups(table[:, WELLS : 2 * WELLS]),
        )
        side_index[side] = product(side_hot[side], 0, side) + product(side_hot[side], 1, side)

    for _, came, dx, z in ties:

        @pl.when(came)
        def _():
            tile_copy(dx, z, gz).wait_recv()

    def scaled(rows, group, d):
        parts = [tiles[4 * group + z] for z in range(4)]
        tile = parts[0] + parts[1] + parts[2] + parts[3]
        sum_p, sum_w = tile[:, 0:WELLS], tile[:, WELLS : 2 * WELLS]
        aim, mode = parts[0][:, 2 * WELLS : 3 * WELLS], parts[0][:, 3 * WELLS : 4 * WELLS]
        bottom = jnp.where(mode == 0.0, (aim + sum_p) / sum_w, aim)
        high, low = split(jnp.concatenate([four(bottom)] * GROUPS, axis=1))
        high, low = rows * high, rows * low
        return bottom, product(high, 0, d) + product(high, 1, d) + product(low, 0, d)

    bottom, values = scaled(own_hot[...], 1, 2)
    hole[...] = bottom
    own_source[...] = values.reshape(L + 2, R, C)
    for side in (0, 1):
        side_source[side] = scaled(side_hot[side], 2 * side, side)[1]

    arrive(near)

    for side in SIDES:
        k = near_end(side)
        p, here = planes(near_in, side, 0), planes(near_in, side, 1)
        across = planes(near_in, side, 4)
        if side % 2:
            across = plane(trans.at[1 if side < 2 else 0], side, k)
        rate = across * jnp.where(has[side], 0.5, 0.0) * (plane(total, side, k) + here)
        border[side] = rate
        add_to_plane(diag, side, k, rate)
        if side < 2:
            well, index = side_source[side], side_index[side]
        else:
            n = L + 1 if side == 2 else L
            well, index = own_source[n], index_sum[n]
        ring[side] = planes(near_in, side, 2) + rate * plane(p0, side, k) + here * (well - p * index)
        over_ring[side] = planes(near_in, side, 3) + rate
        for e, at, c in ends(side):
            cell = corner_in[c]
            if e:
                rate = near_in[side, 80:81]
            else:
                rate = cell[2:3] if side < 2 else cell[3:4]
            rate = rate * jnp.where(has[c // 2] & has[2 + c % 2], 0.5, 0.0)
            rate = rate * (near_in[side, 16 + at : 17 + at] + cell[1:2])
            end_face[2 * side + e] = rate
            ring[side, at : at + 1] += rate * cell[0:1]
            over_ring[side, at : at + 1] += rate
        over_ring[side] = 1.0 / over_ring[side]
        ring[side] *= over_ring[side]
    for c in range(4):
        s, t = c // 2, c % 2
        over_corner[c] = 1.0 / (
            corner_in[c, 4:5] + end_face[2 * s + t] + end_face[2 * (2 + t) + s]
        )

    for l in range(L):
        src = total[l] * (own_source[l] - p0[l] * index_sum[l])
        over = 1.0 / diag[l]
        inverse[l] = over
        source[l] = src
        rhs[l] = storage[l] * p0[l] + src
        first[l] = (num[l] + src) * over
    for side in SIDES:
        k = near_end(side)
        part = border[side] * plane(inverse, side, k)
        weight[side] = part
        add_to_plane(first, side, k, part * planes(near_in, side, 0))

    sent(near)
    for side in SIDES:
        k = 15 - near_end(side)
        behind = 14 if k else 1
        mid_out[side, 0:16] = plane(rhs, side, k)
        for e in (0, 1):
            other = 2 + e if side < 2 else e
            mid_out[side, 16 + e : 17 + e] = weight[other, behind : behind + 1]
    start(mid)

    for l in range(L):
        second[l] = sweep_layer(first, rhs, face, l) * inverse[l]
    for side in SIDES:
        add_to_plane(second, side, near_end(side), weight[side] * ring[side])

    for l in range(L):
        value = sweep_layer(second, rhs, face, l)
        num[l] = value
        third[l] = value * inverse[l]

    sent(bulk)
    for side in SIDES:
        k = 15 - near_end(side)
        behind = 14 if k else 1
        for n, (ref, at) in enumerate(((second, k), (num, k), (third, behind))):
            last_out[side, 16 * n : 16 * n + 16] = plane(ref, side, at)
    for c in range(4):
        k, m = 15 - 15 * (c // 2), 15 - 15 * (c % 2)
        k2, m2 = 14 if k else 1, 14 if m else 1
        last_corner_out[c, 0:1] = second[m, k : k + 1, :]
        last_corner_out[c, 1:2] = num[m, k : k + 1, :]
        last_corner_out[c, 2:3] = second[m, k2 : k2 + 1, :]
        last_corner_out[c, 3:4] = second[m2, k : k + 1, :]
    start(last)

    sent(perf)
    for out, _, dx, z in ties:

        @pl.when(out)
        def _():
            tile_copy(dx, gz, z).wait_send()

    arrive(bulk)

    arrive(mid)
    sent(mid)

    arrive(last)
    sent(last)


def solve(
    storage,
    local,
    frac,
    face,
    inverse,
    rhs,
    source,
    second,
    third,
    border,
    weight,
    over_ring,
    end_face,
    over_corner,
    bulk_in,
    mid_in,
    last_in,
    last_corner_in,
    hole,
    new_p,
    residual,
    new_s,
    new_h,
    new_hole,
    fourth,
    flows,
    out_r,
    out_s,
    out_h,
    sems,
):
    new_hole[...] = hole[...]
    spot = lax.broadcasted_iota(jnp.int32, (16, C), 0)
    corners = []
    for c in range(4):
        s, t = c // 2, c % 2
        value = last_corner_in[c, 1:2]
        value = value + end_face[2 * s + t] * last_in[s, 15 * t : 15 * t + 1]
        value = value + end_face[2 * (2 + t) + s] * last_in[2 + t, 15 * s : 15 * s + 1]
        corners.append(value * over_corner[c])
    rings, parts = [], []
    for side in SIDES:
        k = near_end(side)
        rate = border[side]
        value = planes(last_in, side, 1) + rate * plane(second, side, k)
        behind = planes(last_in, side, 2)
        add = jnp.zeros((16, C), F32)
        for e, at, c in ends(side):
            cell = last_corner_in[c]
            value = value + jnp.where(spot == at, end_face[2 * side + e] * cell[0:1], 0.0)
            far = cell[2:3] if side < 2 else cell[3:4]
            behind = behind + jnp.where(spot == at, mid_in[side, 16 + e : 17 + e] * far, 0.0)
            add = add + jnp.where(spot == at, end_face[2 * side + e] * corners[c], 0.0)
        value = value * over_ring[side]
        rings.append(value)
        along, across, col = (planes(bulk_in, side, n) for n in range(3))
        part = inner_sum(
            planes(mid_in, side, 0) + add, value, behind, None, across, None, along, col
        )
        parts.append(part)
    for side in SIDES:
        add_to_plane(third, side, near_end(side), weight[side] * planes(last_in, side, 0))

    for l in range(L):
        fourth[l] = sweep_layer(third, rhs, face, l) * inverse[l]
    for side in SIDES:
        add_to_plane(fourth, side, near_end(side), weight[side] * rings[side])
    writes = [pltpu.make_async_copy(fourth, new_p, sems.at[0, 3])]
    writes[0].start()
    for side in SIDES:
        k = near_end(side)
        outer = (parts[side] + border[side] * plane(third, side, k)) * over_ring[side]
        flow = border[side] * (plane(fourth, side, k) - outer)
        flows[side, 0] = flow
        flows[side, 1] = flow * jnp.where(flow > 0, plane(frac, side, k), planes(bulk_in, side, 3))

    below = gas_below = None
    for l in range(L):
        p, part = fourth[l], frac[l]
        flow = face[1, l] * (p - shift_rows(p, -1))
        gas = flow * jnp.where(flow > 0, part, shift_rows(part, -1))
        net, out = flow - shift_rows(flow, 1), gas - shift_rows(gas, 1)
        flow = face[2, l] * (p - shift_columns(p, -1))
        gas = flow * jnp.where(flow > 0, part, shift_columns(part, -1))
        net = net + flow - shift_columns(flow, 1)
        out = out + gas - shift_columns(gas, 1)
        for side in (0, 1):
            edge = spot == near_end(side)
            net = net + jnp.where(edge, flows[side, 0, l : l + 1], 0.0)
            out = out + jnp.where(edge, flows[side, 1, l : l + 1], 0.0)
        if l:
            net, out = net - below, out - gas_below
        else:
            net, out = net + flows[2, 0], out + flows[2, 1]
        if l < L - 1:
            below = face[0, l] * (p - fourth[l + 1])
            gas_below = below * jnp.where(below > 0, part, frac[l + 1])
        else:
            below, gas_below = flows[3, 0], flows[3, 1]
        net, out = net + below, out + gas_below
        src = source[l]
        out_r[l] = rhs[l] - storage[l] * p - net
        gas_source = jnp.maximum(src, 0.0) + jnp.minimum(src, 0.0) * part
        saturation = local[0, l] + local[2, l] * (gas_source - out)
        out_s[l] = saturation
        out_h[l] = jnp.maximum(local[1, l], saturation)
        if l % 8 == 7:
            part = pl.ds(l - 7, 8)
            for n, (src, dst) in enumerate(
                ((out_r, residual), (out_s, new_s), (out_h, new_h))
            ):
                copy = pltpu.make_async_copy(src.at[part], dst.at[part], sems.at[l // 8, n])
                copy.start()
                writes.append(copy)
    for copy in writes:
        copy.wait()


def body(
    count_x,
    count_z,
    pressure,
    saturation,
    sat_history,
    storage,
    step_volume,
    transmiss,
    perf_cell,
    perf_index,
    control,
    target,
):
    vmem = pl.BlockSpec(memory_space=pltpu.VMEM)
    hbm = pl.BlockSpec(memory_space=pltpu.HBM)
    dma = pltpu.SemaphoreType.DMA
    block = (L, R, C)
    side = (4, 16, C)
    mid = pl.pallas_call(
        functools.partial(exchange, count_x, count_z),
        out_shape=[
            pltpu.VMEM(shape, F32)
            for shape in (
                block,
                (3, *block),
                block,
                (3, *block),
                *[block] * 5,
                *[side] * 3,
                (8, 1, C),
                (4, 1, C),
                (4, 64, C),
                (4, 24, C),
                (4, 48, C),
                (4, 4, C),
                (1, WELLS),
            )
        ],
        in_specs=[hbm] * 10,
        out_specs=[vmem] * 19,
        scratch_shapes=[
            pltpu.VMEM(block, F32),
            pltpu.VMEM(block, F32),
            pltpu.VMEM((3, *block), F32),
            *[pltpu.VMEM(block, F32)] * 3,
            pltpu.VMEM(side, F32),
            pltpu.VMEM((L + 2, R, C), F32),
            pltpu.VMEM((2, L, C), F32),
            pltpu.VMEM((L + 2, R, C), F32),
            pltpu.VMEM((2, L, C), F32),
            pltpu.VMEM(((L + 2) * R, 512), BF16),
            pltpu.VMEM((2, L, 512), BF16),
            pltpu.VMEM((C, 512), BF16),
            pltpu.VMEM((2, 1536, C), BF16),
            *[pltpu.VMEM((4, 88, C), F32)] * 2,
            *[pltpu.VMEM((4, 8, C), F32)] * 2,
            pltpu.VMEM((4, 64, C), F32),
            pltpu.VMEM((4, 24, C), F32),
            pltpu.VMEM((4, 48, C), F32),
            pltpu.VMEM((4, 4, C), F32),
            pltpu.VMEM((NP, 128), F32),
            pltpu.VMEM((2, NP, 128), F32),
            pltpu.VMEM((1, 128), F32),
            pltpu.VMEM((12, 1, 128), F32),
            pltpu.VMEM((NP, WELLS), jnp.int32),
            pltpu.VMEM((NP, WELLS), F32),
            pltpu.VMEM((1, WELLS), jnp.int32),
            pltpu.VMEM((1, WELLS), F32),
            dma((26,)),
            dma((38,)),
        ],
        compiler_params=pltpu.CompilerParams(
            collective_id=0, has_side_effects=True, vmem_limit_bytes=VMEM_LIMIT
        ),
        name="exchange",
    )(
        *[
            pltpu.with_memory_space_constraint(values, pltpu.HBM)
            for values in (
                pressure,
                saturation,
                sat_history,
                storage,
                step_volume,
                transmiss,
                perf_cell.T,
                perf_index.T,
                control.reshape(1, WELLS),
                target.reshape(1, WELLS),
            )
        ]
    )
    *fields, hole = pl.pallas_call(
        solve,
        out_shape=[jax.ShapeDtypeStruct(block, F32)] * 4
        + [jax.ShapeDtypeStruct((1, WELLS), F32)],
        in_specs=[vmem] * 19,
        out_specs=[hbm] * 4 + [vmem],
        scratch_shapes=[
            pltpu.VMEM(block, F32),
            pltpu.VMEM((4, 2, 16, C), F32),
            *[pltpu.VMEM(block, F32)] * 3,
            dma((2, 4)),
        ],
        compiler_params=pltpu.CompilerParams(vmem_limit_bytes=VMEM_LIMIT),
        name="solve",
    )(*mid)
    return (*fields, hole.reshape(WELLS))


def solution(mesh):
    cells = P("gz", "gx", None)
    return jax.shard_map(
        functools.partial(body, mesh.shape["gx"], mesh.shape["gz"]),
        mesh=mesh,
        in_specs=(
            *[cells] * 5,
            P(None, "gz", "gx", None),
            P("gx", None),
            P("gx", None),
            P("gx"),
            P("gx"),
        ),
        out_specs=(*[cells] * 4, P("gx")),
        check_vma=False,
    )
```

time: 144 us -> 30.9 us (0.21)
  the two profiles are of different devices: /device:TPU:26 before, /device:TPU:24 now
where the time goes in v2:
time: 30.9 us; the launch traced here: 30.7 us
  Pallas kernels  30.1 us (97%)
  between operations  0.64 us (2%)
    pallas_call x1, Pallas kernels, body(): pl.pallas_call(functools.partial(exchange, count_x, count_z), out_shape=[...  27.3 us
    pallas_call x1, Pallas kernels, body(): pl.pallas_call(solve, out_shape=[jax.ShapeDtypeStruct(block, F32)] * 4 +...  2.79 us

profile of v2, /device:TPU:24, one launch (start us, length us, event | category | flops | bytes accessed | tf_op | source)
XLA Modules:
  0.0 30.7 jit_solution(17320142418486213901)
XLA Ops:
  0.6 27.3 %exchange.1 = (f32[16,16,256]{2,1,0:T(8,128)S(1)}, f32[3,16,16,256]{3,2,1,0:T(8,128)S(1)}, f32[16,16,256]{2,1,0:T(8,128)S(1)}, f32[3,16,16,256]{3,2,1,0:T(8,128)...) custom-call(f32[16,16,256]{2,1,0:T(8,128)} %p_in.1, ...), custom_call_target="tpu_custom_call" | custom-call | tf_op jit(solution)/shard_map/exchange/pallas_call | solution.py:738
  27.9 2.8 %solve.1 = (f32[16,16,256]{2,1,0:T(8,128)}, f32[16,16,256]{2,1,0:T(8,128)}, f32[16,16,256]{2,1,0:T(8,128)}, f32[16,16,256]{2,1,0:T(8,128)}, f32[1,32]{1,0:T(1,128)}) custom-call(f32[16,16,256]{2,1,0:T(8,128)S(1)} %get-tuple-element.29.storage, f32[3,16,16,256]{3,2,1,0:T(8,128)S(1)} %get-tuple-element.30.local, f32[16,16,256]{2,1,0:T(8,128)S(1)} %get-tuple-element.31.frac, ...), custom_call_target="tpu_custom_call" | custom-call | tf_op jit(solution)/shard_map/solve/pallas_call | solution.py:812

commit v3 on v2

--- a/solution.py
+++ b/solution.py
@@ -72,13 +72,6 @@
     return jnp.where((layer >= 0) & (layer < L) & (row == (0 if side else R - 1)), layer, -1)
 
 
-def column_values(columns, values):
-    place = lax.broadcasted_iota(jnp.int32, (C, 128), 0)
-    return jnp.concatenate(
-        [jnp.where(place == c, v, 0.0) for c, v in zip(columns, values)], axis=1
-    )
-
-
 def shift_rows(value, by):
     return pltpu.roll(value, by % value.shape[0], 0)
 
@@ -100,6 +93,13 @@
         ref[0:L, k, :] += value
     else:
         ref[k, 0:R, :] += value
+
+
+def set_plane(ref, side, k, value):
+    if side < 2:
+        ref[0:L, k, :] = value
+    else:
+        ref[k, 0:R, :] = value
 
 
 def ends(side):
@@ -150,19 +150,21 @@
     storage,
     local,
     frac,
+    frac_next,
     face,
     inverse,
     rhs,
     source,
     second,
     third,
+    fourth,
     border,
     weight,
     over_ring,
     end_face,
     over_corner,
     bulk_in,
-    mid_in,
+    bulk_out,
     last_in,
     last_corner_in,
     hole,
@@ -178,15 +180,13 @@
     own_source,
     side_source,
     own_hot,
-    side_hot,
     column_hot,
-    spread,
+    columns_own,
+    side_columns,
     near_out,
     near_in,
     corner_out,
     corner_in,
-    bulk_out,
-    mid_out,
     last_out,
     last_corner_out,
     perf_out,
@@ -247,13 +247,12 @@
         @pl.when(jnp.logical_not(has[side]))
         def _():
             near_in[side] = jnp.zeros((88, C), F32)
-            near_in[side, 48:64] = jnp.ones((16, C), F32)
-            bulk_in[side] = jnp.zeros((64, C), F32)
-            mid_in[side] = jnp.zeros((24, C), F32)
-            last_in[side] = jnp.zeros((48, C), F32)
+            near_in[side, 64:80] = jnp.ones((16, C), F32)
+            bulk_in[side] = jnp.zeros((48, C), F32)
+            last_in[side] = jnp.zeros((56, C), F32)
             if side < 2:
                 perf_in[side] = jnp.where(
-                    lax.broadcasted_iota(jnp.int32, (NP, 128), 1) < WELLS, 1e9, 0.0
+                    lax.broadcasted_iota(jnp.int32, (16, 128), 0) < GROUPS, 1e9, 0.0
                 )
                 tiles[8 * side : 8 * side + 4] = jnp.ones((4, 1, 128), F32)
 
@@ -261,7 +260,7 @@
 
         @pl.when(jnp.logical_not(has[c // 2] & has[2 + c % 2]))
         def _():
-            corner_in[c] = jnp.zeros((8, C), F32)
+            corner_in[c] = jnp.zeros((5, C), F32)
             corner_in[c, 4:5] = jnp.ones((1, C), F32)
             last_corner_in[c] = jnp.zeros((4, C), F32)
 
@@ -275,8 +274,10 @@
         part = slice(128 * g, 128 * g + 128)
         own_hot[:, part] = one_hot((L + 2) * R, own_row[g]).astype(BF16)
         column_hot[:, part] = one_hot(C, own_column[g]).astype(BF16)
-    table = jnp.concatenate([pc[...].astype(F32), pi[...]], axis=1)
-    perf_out[...] = jnp.concatenate([table, table], axis=1)
+    for side in (0, 1):
+        for g in range(GROUPS):
+            perf_out[side, g : g + 1] = cell[g].astype(F32)
+            perf_out[side, GROUPS + g : GROUPS + g + 1] = own_index[g]
 
     for n in (2, 3):
         loads[n].wait()
@@ -320,17 +321,17 @@
     for side in SIDES:
         k = 15 - near_end(side)
         normal, along = (1, 0) if side < 2 else (0, 1)
-        for n, ref in enumerate((p0, total, num, diag, trans.at[normal])):
+        for n, ref in enumerate((p0, total, trans.at[normal], num, diag)):
             near_out[side, 16 * n : 16 * n + 16] = plane(ref, side, k)
         if side < 2:
-            near_out[side, 80:81] = trans[along, L - 1, k : k + 1, :]
+            for h in (0, 1):
+                perf_out[side, 8 + h : 9 + h] = trans[
+                    along, L - 1, k : k + 1, 128 * h : 128 * h + 128
+                ]
         else:
             near_out[side, 80:81] = trans[along, k, R - 1 : R, :]
-        behind = min(k, 14)
-        for n, (ref, at) in enumerate(
-            ((face.at[along], k), (face.at[normal], behind), (face.at[2], k), (frac, k))
-        ):
-            bulk_out[side, 16 * n : 16 * n + 16] = plane(ref, side, at)
+        for n, ref in enumerate((face.at[along], face.at[2], frac)):
+            bulk_out[side, 16 * n : 16 * n + 16] = plane(ref, side, k)
     for c in range(4):
         k, m = 15 - 15 * (c // 2), 15 - 15 * (c % 2)
         for n, ref in enumerate((p0, total, trans.at[0], trans.at[1], diag)):
@@ -378,7 +379,7 @@
             device_id_type=MESH,
         )
 
-    near, perf, bulk, mid, last = [], [], [], [], []
+    front, near, perf, bulk, last = [], [], [], [], []
     for c in range(4):
         s, t = c // 2, 2 + c % 2
         ok = (has[s ^ 1] & has[t ^ 1], has[s] & has[t])
@@ -387,13 +388,20 @@
         last.append((*ok, remote(last_corner_out.at[c], last_corner_in.at[c], 4 + c, 18 + c, to)))
     for side in SIDES:
         ok, to = (has[side ^ 1], has[side]), target(side)
-        near.append((*ok, remote(near_out.at[side], near_in.at[side], side, side, to)))
-        bulk.append((*ok, remote(bulk_out.at[side], bulk_in.at[side], 22 + side, 10 + side, to)))
-        mid.append((*ok, remote(mid_out.at[side], mid_in.at[side], side, 34 + side, to)))
-        last.append((*ok, remote(last_out.at[side], last_in.at[side], 22 + side, 14 + side, to)))
+        rows = pl.ds(0, (48, 32, 88, 88)[side])
+        copy = remote(near_out.at[side, rows], near_in.at[side, rows], side, side, to)
+        (front if side < 2 else near).append((*ok, copy))
+        if side < 2:
+            rows = pl.ds(48, 32)
+            copy = remote(
+                near_out.at[side, rows], near_in.at[side, rows], 13 + side, 25 + side, to
+            )
+            near.append((*ok, copy))
+        bulk.append((*ok, remote(bulk_out.at[side], bulk_in.at[side], 15 + side, 10 + side, to)))
+        last.append((*ok, remote(last_out.at[side], last_in.at[side], 19 + side, 14 + side, to)))
     for side in (0, 1):
         ok, to = (has[side ^ 1], has[side]), target(side)
-        perf.append((*ok, remote(perf_out, perf_in.at[side], 8 + side, 8 + side, to)))
+        perf.append((*ok, remote(perf_out.at[side], perf_in.at[side], 8 + side, 8 + side, to)))
 
     def start(copies):
         for out, _, copy in copies:
@@ -420,8 +428,8 @@
         return pltpu.make_async_remote_copy(
             src_ref=tile_out,
             dst_ref=tiles.at[4 * (1 - dx) + z_from],
-            send_sem=send_sem.at[10 + 4 * (1 - dx) + z_to],
-            recv_sem=recv_sem.at[22 + 4 * (1 - dx) + z_from],
+            send_sem=send_sem.at[11 - dx],
+            recv_sem=recv_sem.at[23 - dx],
             device_id=(gx + dx, z_to),
             device_id_type=MESH,
         )
@@ -441,82 +449,133 @@
         def _():
             tile_copy(dx, gz, z).start()
 
+    start(front)
     start(near)
 
+
+    def stacked(values):
+        return jnp.concatenate(split(values), axis=0)
+
+    def halves(values):
+        n = values.shape[0] // 2
+        return values[0:n] + values[n:]
+
+    own_flat = jnp.concatenate(own_index, axis=1)
+    columns_own[...] = jnp.concatenate([one_hot(C, c) for c in own_column], axis=1).T.astype(BF16)
+
+    def own_scatter(values):
+        high, low = split(values)
+        rows = jnp.concatenate([own_hot[...] * high, own_hot[...] * low], axis=0)
+        found = jnp.dot(rows, columns_own[...], preferred_element_type=F32)
+        return halves(found).reshape(L + 2, R, C)
+
+    index_sum[...] = own_scatter(own_flat)
+    def group_wait(dx, sem):
+        some = tiles.at[pl.ds(0, 4 if dx else 3)]
+        pltpu.make_async_copy(some, some, sem).wait()
+
+    def bottoms(groups):
+        parts = [[tiles[4 * group + z] for z in range(4)] for group in groups]
+        tile = jnp.concatenate([a + b + c + d for a, b, c, d in parts], axis=0)
+        given = jnp.concatenate([group[0] for group in parts], axis=0)
+        aim, mode = pltpu.roll(given, 64, 1), pltpu.roll(given, 32, 1)
+        bottom = jnp.where(mode == 0.0, (aim + tile) / pltpu.roll(tile, 96, 1), aim)
+        quarter = lax.broadcasted_iota(jnp.int32, bottom.shape, 1) // WELLS
+        bottom = jnp.where(quarter == 0, bottom, 0.0)
+        bottom = bottom + pltpu.roll(bottom, 64, 1)
+        bottom = bottom + pltpu.roll(bottom, 32, 1)
+        return jnp.concatenate([bottom] * GROUPS, axis=1)
+
+    group_wait(0, recv_sem.at[23])
+
+    bottom = bottoms([1])
+    hole[...] = bottom[:, 0:WELLS]
+    own_source[...] = own_scatter(own_flat * bottom)
+
+    for l in range(L):
+        src = total[l] * (own_source[l] - p0[l] * index_sum[l])
+        over = 1.0 / diag[l]
+        value = num[l] + src
+        source[l] = src
+        rhs[l] = storage[l] * p0[l] + src
+        num[l] = value
+        inverse[l] = over
+        first[l] = value * over
+
+    arrive(perf)
     start(bulk)
 
-    def place_index(d, columns, indices):
-        high, low = split(column_values(columns, indices).T)
-        spread[0, 512 * d : 512 * d + 512, :] = high
-        spread[1, 512 * d : 512 * d + 512, :] = low
-
-    def product(rows, n, d):
-        return jnp.dot(
-            rows, spread[n, 512 * d : 512 * d + 512, :], preferred_element_type=F32
+    side_rates = []
+    for side in (0, 1):
+        cell = [perf_in[side, g : g + 1].astype(jnp.int32) for g in range(GROUPS)]
+        index = [perf_in[side, GROUPS + g : GROUPS + g + 1] for g in range(GROUPS)]
+        rates = [one_hot(L, side_rows(v, gz, side)) * i for v, i in zip(cell, index)]
+        side_rates.append(jnp.concatenate(rates, axis=1))
+        for g in range(GROUPS):
+            part = slice(128 * g, 128 * g + 128)
+            side_columns[side, :, part] = one_hot(C, cell_parts(cell[g], gz)[2]).astype(BF16)
+
+    for dx in (1, -1):
+
+        @pl.when(has[0 if dx > 0 else 1])
+        def _():
+            group_wait(dx, recv_sem.at[23 - dx])
+
+    bottom = bottoms([0, 2])
+    for side in (0, 1):
+        rates = side_rates[side]
+        found = lax.dot_general(
+            side_columns[side],
+            stacked(jnp.concatenate([rates, rates * bottom[side : side + 1]], axis=0)),
+            (((1,), (1,)), ((), ())),
+            preferred_element_type=F32,
         )
-
-    place_index(2, own_column, own_index)
-    index_sum[...] = (product(own_hot[...], 0, 2) + product(own_hot[...], 1, 2)).reshape(
-        L + 2, R, C
-    )
-    arrive(perf)
-    for side in (0, 1):
-        table = perf_in[side]
-        cell = lane_groups(table[:, 0:WELLS].astype(jnp.int32))
-        for g in range(GROUPS):
-            side_hot[side, :, 128 * g : 128 * g + 128] = one_hot(
-                L, side_rows(cell[g], gz, side)
-            ).astype(BF16)
-        place_index(
-            side,
-            [cell_parts(v, gz)[2] for v in cell],
-            lane_groups(table[:, WELLS : 2 * WELLS]),
-        )
-        side_index[side] = product(side_hot[side], 0, side) + product(side_hot[side], 1, side)
-
-    for _, came, dx, z in ties:
-
-        @pl.when(came)
-        def _():
-            tile_copy(dx, z, gz).wait_recv()
-
-    def scaled(rows, group, d):
-        parts = [tiles[4 * group + z] for z in range(4)]
-        tile = parts[0] + parts[1] + parts[2] + parts[3]
-        sum_p, sum_w = tile[:, 0:WELLS], tile[:, WELLS : 2 * WELLS]
-        aim, mode = parts[0][:, 2 * WELLS : 3 * WELLS], parts[0][:, 3 * WELLS : 4 * WELLS]
-        bottom = jnp.where(mode == 0.0, (aim + sum_p) / sum_w, aim)
-        high, low = split(jnp.concatenate([four(bottom)] * GROUPS, axis=1))
-        high, low = rows * high, rows * low
-        return bottom, product(high, 0, d) + product(high, 1, d) + product(low, 0, d)
-
-    bottom, values = scaled(own_hot[...], 1, 2)
-    hole[...] = bottom
-    own_source[...] = values.reshape(L + 2, R, C)
-    for side in (0, 1):
-        side_source[side] = scaled(side_hot[side], 2 * side, side)[1]
-
-    arrive(near)
+        found = halves(found.T)
+        side_index[side] = found[0:L]
+        side_source[side] = found[L:]
+
+    arrive(front)
+    arrive(near[-2:])
+
+    for side in SIDES:
+        k = near_end(side)
+        across = planes(near_in, side, 2)
+        if side % 2:
+            across = plane(trans.at[1 if side < 2 else 0], side, k)
+        rate = plane(total, side, k) + planes(near_in, side, 1)
+        rate = rate * across * jnp.where(has[side], 0.5, 0.0)
+        border[side] = rate
+        add_to_plane(diag, side, k, rate)
+        add_to_plane(num, side, k, rate * planes(near_in, side, 0))
+
+    for side in SIDES:
+        k = near_end(side)
+        over = 1.0 / plane(diag, side, k)
+        set_plane(inverse, side, k, over)
+        set_plane(first, side, k, plane(num, side, k) * over)
+        weight[side] = border[side] * over
+
+    for l in range(L):
+        second[l] = sweep_layer(first, rhs, face, l) * inverse[l]
+
+    arrive(near[:-2])
 
     for side in SIDES:
         k = near_end(side)
         p, here = planes(near_in, side, 0), planes(near_in, side, 1)
-        across = planes(near_in, side, 4)
-        if side % 2:
-            across = plane(trans.at[1 if side < 2 else 0], side, k)
-        rate = across * jnp.where(has[side], 0.5, 0.0) * (plane(total, side, k) + here)
-        border[side] = rate
-        add_to_plane(diag, side, k, rate)
         if side < 2:
             well, index = side_source[side], side_index[side]
         else:
             n = L + 1 if side == 2 else L
             well, index = own_source[n], index_sum[n]
-        ring[side] = planes(near_in, side, 2) + rate * plane(p0, side, k) + here * (well - p * index)
-        over_ring[side] = planes(near_in, side, 3) + rate
+        value = planes(near_in, side, 3) + border[side] * plane(p0, side, k)
+        ring[side] = value + here * (well - p * index)
+        over_ring[side] = planes(near_in, side, 4) + border[side]
         for e, at, c in ends(side):
             cell = corner_in[c]
-            if e:
+            if e and side < 2:
+                rate = jnp.concatenate([perf_in[side, 8:9], perf_in[side, 9:10]], axis=1)
+            elif e:
                 rate = near_in[side, 80:81]
             else:
                 rate = cell[2:3] if side < 2 else cell[3:4]
@@ -526,7 +585,7 @@
             ring[side, at : at + 1] += rate * cell[0:1]
             over_ring[side, at : at + 1] += rate
         over_ring[side] = 1.0 / over_ring[side]
-        ring[side] *= over_ring[side]
+        add_to_plane(second, side, k, weight[side] * (ring[side] * over_ring[side]))
     for c in range(4):
         s, t = c // 2, c % 2
         over_corner[c] = 1.0 / (
@@ -534,44 +593,22 @@
         )
 
     for l in range(L):
-        src = total[l] * (own_source[l] - p0[l] * index_sum[l])
-        over = 1.0 / diag[l]
-        inverse[l] = over
-        source[l] = src
-        rhs[l] = storage[l] * p0[l] + src
-        first[l] = (num[l] + src) * over
-    for side in SIDES:
-        k = near_end(side)
-        part = border[side] * plane(inverse, side, k)
-        weight[side] = part
-        add_to_plane(first, side, k, part * planes(near_in, side, 0))
-
-    sent(near)
-    for side in SIDES:
-        k = 15 - near_end(side)
-        behind = 14 if k else 1
-        mid_out[side, 0:16] = plane(rhs, side, k)
-        for e in (0, 1):
-            other = 2 + e if side < 2 else e
-            mid_out[side, 16 + e : 17 + e] = weight[other, behind : behind + 1]
-    start(mid)
-
-    for l in range(L):
-        second[l] = sweep_layer(first, rhs, face, l) * inverse[l]
-    for side in SIDES:
-        add_to_plane(second, side, near_end(side), weight[side] * ring[side])
-
-    for l in range(L):
         value = sweep_layer(second, rhs, face, l)
         num[l] = value
         third[l] = value * inverse[l]
 
-    sent(bulk)
     for side in SIDES:
         k = 15 - near_end(side)
         behind = 14 if k else 1
-        for n, (ref, at) in enumerate(((second, k), (num, k), (third, behind))):
-            last_out[side, 16 * n : 16 * n + 16] = plane(ref, side, at)
+        across = plane(face.at[1 if side < 2 else 0], side, min(k, 14))
+        last_out[side, 0:16] = plane(second, side, k)
+        last_out[side, 16:32] = plane(num, side, k)
+        last_out[side, 32:48] = plane(rhs, side, k) + across * plane(third, side, behind)
+        for e in (0, 1):
+            other = 2 + e if side < 2 else e
+            last_out[side, 48 + e : 49 + e] = (
+                weight[other, behind : behind + 1] * across[15 * e : 15 * e + 1]
+            )
     for c in range(4):
         k, m = 15 - 15 * (c // 2), 15 - 15 * (c % 2)
         k2, m2 = 14 if k else 1, 14 if m else 1
@@ -579,19 +616,31 @@
         last_corner_out[c, 1:2] = num[m, k : k + 1, :]
         last_corner_out[c, 2:3] = second[m, k2 : k2 + 1, :]
         last_corner_out[c, 3:4] = second[m2, k : k + 1, :]
+    sent(front)
+    sent(near)
     start(last)
 
+    for l in range(L):
+        fourth[l] = sweep_layer(third, rhs, face, l) * inverse[l]
+
+    for l in range(L):
+        src, part = source[l], frac[l]
+        gas_source = jnp.maximum(src, 0.0) + jnp.minimum(src, 0.0) * part
+        source[l] = local[0, l] + local[2, l] * gas_source
+        frac_next[0, l] = shift_rows(part, -1)
+        frac_next[1, l] = shift_columns(part, -1)
+
     sent(perf)
-    for out, _, dx, z in ties:
+    for dx in (1, -1, 0):
+        out = True if dx == 0 else has[1 if dx > 0 else 0]
 
         @pl.when(out)
         def _():
-            tile_copy(dx, gz, z).wait_send()
+            group_wait(dx, send_sem.at[11 - dx])
 
     arrive(bulk)
-
-    arrive(mid)
-    sent(mid)
+    sent(bulk)
+
 
     arrive(last)
     sent(last)
@@ -601,19 +650,21 @@
     storage,
     local,
     frac,
+    frac_next,
     face,
     inverse,
     rhs,
     source,
     second,
     third,
+    fourth,
     border,
     weight,
     over_ring,
     end_face,
     over_corner,
     bulk_in,
-    mid_in,
+    bulk_out,
     last_in,
     last_corner_in,
     hole,
@@ -622,7 +673,6 @@
     new_s,
     new_h,
     new_hole,
-    fourth,
     flows,
     out_r,
     out_s,
@@ -643,51 +693,56 @@
         k = near_end(side)
         rate = border[side]
         value = planes(last_in, side, 1) + rate * plane(second, side, k)
-        behind = planes(last_in, side, 2)
-        add = jnp.zeros((16, C), F32)
+        add = planes(last_in, side, 2)
         for e, at, c in ends(side):
             cell = last_corner_in[c]
             value = value + jnp.where(spot == at, end_face[2 * side + e] * cell[0:1], 0.0)
             far = cell[2:3] if side < 2 else cell[3:4]
-            behind = behind + jnp.where(spot == at, mid_in[side, 16 + e : 17 + e] * far, 0.0)
+            add = add + jnp.where(spot == at, last_in[side, 48 + e : 49 + e] * far, 0.0)
             add = add + jnp.where(spot == at, end_face[2 * side + e] * corners[c], 0.0)
         value = value * over_ring[side]
         rings.append(value)
-        along, across, col = (planes(bulk_in, side, n) for n in range(3))
-        part = inner_sum(
-            planes(mid_in, side, 0) + add, value, behind, None, across, None, along, col
-        )
-        parts.append(part)
-    for side in SIDES:
-        add_to_plane(third, side, near_end(side), weight[side] * planes(last_in, side, 0))
-
-    for l in range(L):
-        fourth[l] = sweep_layer(third, rhs, face, l) * inverse[l]
-    for side in SIDES:
-        add_to_plane(fourth, side, near_end(side), weight[side] * rings[side])
+        along, col = planes(bulk_in, side, 0), planes(bulk_in, side, 1)
+        parts.append(inner_sum(add, value, None, None, None, None, along, col))
+    for side in SIDES:
+        k = near_end(side)
+        behind = 14 if k else 1
+        change = weight[side] * planes(last_in, side, 0)
+        add_to_plane(third, side, k, change)
+        along, col = planes(bulk_out, side ^ 1, 0), planes(bulk_out, side ^ 1, 1)
+        across = plane(face.at[1 if side < 2 else 0], side, min(k, 14))
+        value = inner_sum(border[side] * rings[side], change, None, None, None, None, along, col)
+        add_to_plane(fourth, side, k, value * plane(inverse, side, k))
+        add_to_plane(fourth, side, behind, across * change * plane(inverse, side, behind))
+
     writes = [pltpu.make_async_copy(fourth, new_p, sems.at[0, 3])]
     writes[0].start()
     for side in SIDES:
         k = near_end(side)
         outer = (parts[side] + border[side] * plane(third, side, k)) * over_ring[side]
-        flow = border[side] * (plane(fourth, side, k) - outer)
+        rate = -border[side] if side == 0 else border[side]
+        flow = rate * (plane(fourth, side, k) - outer)
         flows[side, 0] = flow
-        flows[side, 1] = flow * jnp.where(flow > 0, plane(frac, side, k), planes(bulk_in, side, 3))
-
+        flows[side, 1] = flow * jnp.where(
+            (flow < 0) if side == 0 else (flow > 0),
+            planes(bulk_out, side ^ 1, 2),
+            planes(bulk_in, side, 2),
+        )
+
+    first_row, last_row = spot == 0, spot == R - 1
     below = gas_below = None
     for l in range(L):
         p, part = fourth[l], frac[l]
         flow = face[1, l] * (p - shift_rows(p, -1))
-        gas = flow * jnp.where(flow > 0, part, shift_rows(part, -1))
-        net, out = flow - shift_rows(flow, 1), gas - shift_rows(gas, 1)
+        gas = flow * jnp.where(flow > 0, part, frac_next[0, l])
+        flow = jnp.where(last_row, flows[1, 0, l : l + 1], flow)
+        gas = jnp.where(last_row, flows[1, 1, l : l + 1], gas)
+        net = flow - jnp.where(first_row, flows[0, 0, l : l + 1], shift_rows(flow, 1))
+        out = gas - jnp.where(first_row, flows[0, 1, l : l + 1], shift_rows(gas, 1))
         flow = face[2, l] * (p - shift_columns(p, -1))
-        gas = flow * jnp.where(flow > 0, part, shift_columns(part, -1))
+        gas = flow * jnp.where(flow > 0, part, frac_next[1, l])
         net = net + flow - shift_columns(flow, 1)
         out = out + gas - shift_columns(gas, 1)
-        for side in (0, 1):
-            edge = spot == near_end(side)
-            net = net + jnp.where(edge, flows[side, 0, l : l + 1], 0.0)
-            out = out + jnp.where(edge, flows[side, 1, l : l + 1], 0.0)
         if l:
             net, out = net - below, out - gas_below
         else:
@@ -698,10 +753,8 @@
         else:
             below, gas_below = flows[3, 0], flows[3, 1]
         net, out = net + below, out + gas_below
-        src = source[l]
         out_r[l] = rhs[l] - storage[l] * p - net
-        gas_source = jnp.maximum(src, 0.0) + jnp.minimum(src, 0.0) * part
-        saturation = local[0, l] + local[2, l] * (gas_source - out)
+        saturation = source[l] - local[2, l] * out
         out_s[l] = saturation
         out_h[l] = jnp.maximum(local[1, l], saturation)
         if l % 8 == 7:
@@ -743,20 +796,20 @@
                 block,
                 (3, *block),
                 block,
+                (2, *block),
                 (3, *block),
-                *[block] * 5,
+                *[block] * 6,
                 *[side] * 3,
                 (8, 1, C),
                 (4, 1, C),
-                (4, 64, C),
-                (4, 24, C),
-                (4, 48, C),
+                *[(4, 48, C)] * 2,
+                (4, 56, C),
                 (4, 4, C),
                 (1, WELLS),
             )
         ],
         in_specs=[hbm] * 10,
-        out_specs=[vmem] * 19,
+        out_specs=[vmem] * 21,
         scratch_shapes=[
             pltpu.VMEM(block, F32),
             pltpu.VMEM(block, F32),
@@ -768,25 +821,22 @@
             pltpu.VMEM((L + 2, R, C), F32),
             pltpu.VMEM((2, L, C), F32),
             pltpu.VMEM(((L + 2) * R, 512), BF16),
-            pltpu.VMEM((2, L, 512), BF16),
             pltpu.VMEM((C, 512), BF16),
-            pltpu.VMEM((2, 1536, C), BF16),
+            pltpu.VMEM((512, C), BF16),
+            pltpu.VMEM((2, C, 512), BF16),
             *[pltpu.VMEM((4, 88, C), F32)] * 2,
-            *[pltpu.VMEM((4, 8, C), F32)] * 2,
-            pltpu.VMEM((4, 64, C), F32),
-            pltpu.VMEM((4, 24, C), F32),
-            pltpu.VMEM((4, 48, C), F32),
+            *[pltpu.VMEM((4, 5, C), F32)] * 2,
+            pltpu.VMEM((4, 56, C), F32),
             pltpu.VMEM((4, 4, C), F32),
-            pltpu.VMEM((NP, 128), F32),
-            pltpu.VMEM((2, NP, 128), F32),
+            *[pltpu.VMEM((2, 16, 128), F32)] * 2,
             pltpu.VMEM((1, 128), F32),
             pltpu.VMEM((12, 1, 128), F32),
             pltpu.VMEM((NP, WELLS), jnp.int32),
             pltpu.VMEM((NP, WELLS), F32),
             pltpu.VMEM((1, WELLS), jnp.int32),
             pltpu.VMEM((1, WELLS), F32),
-            dma((26,)),
-            dma((38,)),
+            dma((23,)),
+            dma((27,)),
         ],
         compiler_params=pltpu.CompilerParams(
             collective_id=0, has_side_effects=True, vmem_limit_bytes=VMEM_LIMIT
@@ -813,10 +863,9 @@
         solve,
         out_shape=[jax.ShapeDtypeStruct(block, F32)] * 4
         + [jax.ShapeDtypeStruct((1, WELLS), F32)],
-        in_specs=[vmem] * 19,
+        in_specs=[vmem] * 21,
         out_specs=[hbm] * 4 + [vmem],
         scratch_shapes=[
-            pltpu.VMEM(block, F32),
             pltpu.VMEM((4, 2, 16, C), F32),
             *[pltpu.VMEM(block, F32)] * 3,
             dma((2, 4)),

time: 30.9 us -> 28.5 us (0.922)
  Pallas kernels: 30.1 us -> 27.7 us
    pallas_call x1, Pallas kernels: 27.3 us -> 25.5 us  [body(): pl.pallas_call(functools.partial(exchange, count_x, count_z), out_shape=[...]
    pallas_call x1, Pallas kernels: 2.79 us -> 2.18 us  [body(): pl.pallas_call(solve, out_shape=[jax.ShapeDtypeStruct(block, F32)] * 4 +...]
where the time goes in v3:
time: 28.5 us; the launch traced here: 28.3 us
  Pallas kernels  27.7 us (97%)
  between operations  0.64 us (2%)
    pallas_call x1, Pallas kernels, body(): pl.pallas_call(functools.partial(exchange, count_x, count_z), out_shape=[...  25.5 us
    pallas_call x1, Pallas kernels, body(): pl.pallas_call(solve, out_shape=[jax.ShapeDtypeStruct(block, F32)] * 4 +...  2.18 us

profile of v3, /device:TPU:24, one launch (start us, length us, event | category | flops | bytes accessed | tf_op | source)
XLA Modules:
  0.0 28.3 jit_solution(1032658882064977667)
XLA Ops:
  0.6 25.5 %exchange.1 = (f32[16,16,256]{2,1,0:T(8,128)S(1)}, f32[3,16,16,256]{3,2,1,0:T(8,128)S(1)}, f32[16,16,256]{2,1,0:T(8,128)S(1)}, f32[2,16,16,256]{3,2,1,0:T(8,128)...) custom-call(f32[16,16,256]{2,1,0:T(8,128)} %p_in.1, ...), custom_call_target="tpu_custom_call" | custom-call | tf_op jit(solution)/shard_map/exchange/pallas_call | solution.py:791
  26.1 2.2 %solve.1 = (f32[16,16,256]{2,1,0:T(8,128)}, f32[16,16,256]{2,1,0:T(8,128)}, f32[16,16,256]{2,1,0:T(8,128)}, f32[16,16,256]{2,1,0:T(8,128)}, f32[1,32]{1,0:T(1,128)}) custom-call(f32[16,16,256]{2,1,0:T(8,128)S(1)} %get-tuple-element.31.storage, f32[3,16,16,256]{3,2,1,0:T(8,128)S(1)} %get-tuple-element.32.local, f32[16,16,256]{2,1,0:T(8,128)S(1)} %get-tuple-element.33.frac, ...), custom_call_target="tpu_custom_call" | custom-call | tf_op jit(solution)/shard_map/solve/pallas_call | solution.py:862

commit v4 on v3

--- a/solution.py
+++ b/solution.py
@@ -165,6 +165,7 @@
     over_corner,
     bulk_in,
     bulk_out,
+    mid_in,
     last_in,
     last_corner_in,
     hole,
@@ -187,6 +188,7 @@
     near_in,
     corner_out,
     corner_in,
+    mid_out,
     last_out,
     last_corner_out,
     perf_out,
@@ -249,7 +251,8 @@
             near_in[side] = jnp.zeros((88, C), F32)
             near_in[side, 64:80] = jnp.ones((16, C), F32)
             bulk_in[side] = jnp.zeros((48, C), F32)
-            last_in[side] = jnp.zeros((56, C), F32)
+            mid_in[side] = jnp.zeros((24, C), F32)
+            last_in[side] = jnp.zeros((32, C), F32)
             if side < 2:
                 perf_in[side] = jnp.where(
                     lax.broadcasted_iota(jnp.int32, (16, 128), 0) < GROUPS, 1e9, 0.0
@@ -379,7 +382,7 @@
             device_id_type=MESH,
         )
 
-    front, near, perf, bulk, last = [], [], [], [], []
+    front, near, perf, bulk, mid, last = [], [], [], [], [], []
     for c in range(4):
         s, t = c // 2, 2 + c % 2
         ok = (has[s ^ 1] & has[t ^ 1], has[s] & has[t])
@@ -398,6 +401,7 @@
             )
             near.append((*ok, copy))
         bulk.append((*ok, remote(bulk_out.at[side], bulk_in.at[side], 15 + side, 10 + side, to)))
+        mid.append((*ok, remote(mid_out.at[side], mid_in.at[side], side, 27 + side, to)))
         last.append((*ok, remote(last_out.at[side], last_in.at[side], 19 + side, 14 + side, to)))
     for side in (0, 1):
         ok, to = (has[side ^ 1], has[side]), target(side)
@@ -592,6 +596,20 @@
             corner_in[c, 4:5] + end_face[2 * s + t] + end_face[2 * (2 + t) + s]
         )
 
+    sent(front)
+    sent(near)
+    for side in SIDES:
+        k = 15 - near_end(side)
+        behind = 14 if k else 1
+        across = plane(face.at[1 if side < 2 else 0], side, min(k, 14))
+        mid_out[side, 0:16] = plane(second, side, k)
+        for e in (0, 1):
+            other = 2 + e if side < 2 else e
+            mid_out[side, 16 + e : 17 + e] = (
+                weight[other, behind : behind + 1] * across[15 * e : 15 * e + 1]
+            )
+    start(mid)
+
     for l in range(L):
         value = sweep_layer(second, rhs, face, l)
         num[l] = value
@@ -601,14 +619,8 @@
         k = 15 - near_end(side)
         behind = 14 if k else 1
         across = plane(face.at[1 if side < 2 else 0], side, min(k, 14))
-        last_out[side, 0:16] = plane(second, side, k)
-        last_out[side, 16:32] = plane(num, side, k)
-        last_out[side, 32:48] = plane(rhs, side, k) + across * plane(third, side, behind)
-        for e in (0, 1):
-            other = 2 + e if side < 2 else e
-            last_out[side, 48 + e : 49 + e] = (
-                weight[other, behind : behind + 1] * across[15 * e : 15 * e + 1]
-            )
+        last_out[side, 0:16] = plane(num, side, k)
+        last_out[side, 16:32] = plane(rhs, side, k) + across * plane(third, side, behind)
     for c in range(4):
         k, m = 15 - 15 * (c // 2), 15 - 15 * (c % 2)
         k2, m2 = 14 if k else 1, 14 if m else 1
@@ -616,8 +628,6 @@
         last_corner_out[c, 1:2] = num[m, k : k + 1, :]
         last_corner_out[c, 2:3] = second[m, k2 : k2 + 1, :]
         last_corner_out[c, 3:4] = second[m2, k : k + 1, :]
-    sent(front)
-    sent(near)
     start(last)
 
     for l in range(L):
@@ -641,6 +651,9 @@
     arrive(bulk)
     sent(bulk)
 
+
+    arrive(mid)
+    sent(mid)
 
     arrive(last)
     sent(last)
@@ -665,6 +678,7 @@
     over_corner,
     bulk_in,
     bulk_out,
+    mid_in,
     last_in,
     last_corner_in,
     hole,
@@ -679,26 +693,27 @@
     out_h,
     sems,
 ):
-    new_hole[...] = hole[...]
+    writes = [pltpu.make_async_copy(hole, new_hole, sems.at[1, 3])]
+    writes[0].start()
     spot = lax.broadcasted_iota(jnp.int32, (16, C), 0)
     corners = []
     for c in range(4):
         s, t = c // 2, c % 2
         value = last_corner_in[c, 1:2]
-        value = value + end_face[2 * s + t] * last_in[s, 15 * t : 15 * t + 1]
-        value = value + end_face[2 * (2 + t) + s] * last_in[2 + t, 15 * s : 15 * s + 1]
+        value = value + end_face[2 * s + t] * mid_in[s, 15 * t : 15 * t + 1]
+        value = value + end_face[2 * (2 + t) + s] * mid_in[2 + t, 15 * s : 15 * s + 1]
         corners.append(value * over_corner[c])
     rings, parts = [], []
     for side in SIDES:
         k = near_end(side)
         rate = border[side]
-        value = planes(last_in, side, 1) + rate * plane(second, side, k)
-        add = planes(last_in, side, 2)
+        value = planes(last_in, side, 0) + rate * plane(second, side, k)
+        add = planes(last_in, side, 1)
         for e, at, c in ends(side):
             cell = last_corner_in[c]
             value = value + jnp.where(spot == at, end_face[2 * side + e] * cell[0:1], 0.0)
             far = cell[2:3] if side < 2 else cell[3:4]
-            add = add + jnp.where(spot == at, last_in[side, 48 + e : 49 + e] * far, 0.0)
+            add = add + jnp.where(spot == at, mid_in[side, 16 + e : 17 + e] * far, 0.0)
             add = add + jnp.where(spot == at, end_face[2 * side + e] * corners[c], 0.0)
         value = value * over_ring[side]
         rings.append(value)
@@ -707,7 +722,7 @@
     for side in SIDES:
         k = near_end(side)
         behind = 14 if k else 1
-        change = weight[side] * planes(last_in, side, 0)
+        change = weight[side] * planes(mid_in, side, 0)
         add_to_plane(third, side, k, change)
         along, col = planes(bulk_out, side ^ 1, 0), planes(bulk_out, side ^ 1, 1)
         across = plane(face.at[1 if side < 2 else 0], side, min(k, 14))
@@ -715,8 +730,8 @@
         add_to_plane(fourth, side, k, value * plane(inverse, side, k))
         add_to_plane(fourth, side, behind, across * change * plane(inverse, side, behind))
 
-    writes = [pltpu.make_async_copy(fourth, new_p, sems.at[0, 3])]
-    writes[0].start()
+    writes.append(pltpu.make_async_copy(fourth, new_p, sems.at[0, 3]))
+    writes[1].start()
     for side in SIDES:
         k = near_end(side)
         outer = (parts[side] + border[side] * plane(third, side, k)) * over_ring[side]
@@ -803,13 +818,14 @@
                 (8, 1, C),
                 (4, 1, C),
                 *[(4, 48, C)] * 2,
-                (4, 56, C),
+                (4, 24, C),
+                (4, 32, C),
                 (4, 4, C),
                 (1, WELLS),
             )
         ],
         in_specs=[hbm] * 10,
-        out_specs=[vmem] * 21,
+        out_specs=[vmem] * 22,
         scratch_shapes=[
             pltpu.VMEM(block, F32),
             pltpu.VMEM(block, F32),
@@ -826,7 +842,8 @@
             pltpu.VMEM((2, C, 512), BF16),
             *[pltpu.VMEM((4, 88, C), F32)] * 2,
             *[pltpu.VMEM((4, 5, C), F32)] * 2,
-            pltpu.VMEM((4, 56, C), F32),
+            pltpu.VMEM((4, 24, C), F32),
+            pltpu.VMEM((4, 32, C), F32),
             pltpu.VMEM((4, 4, C), F32),
             *[pltpu.VMEM((2, 16, 128), F32)] * 2,
             pltpu.VMEM((1, 128), F32),
@@ -836,7 +853,7 @@
             pltpu.VMEM((1, WELLS), jnp.int32),
             pltpu.VMEM((1, WELLS), F32),
             dma((23,)),
-            dma((27,)),
+            dma((31,)),
         ],
         compiler_params=pltpu.CompilerParams(
             collective_id=0, has_side_effects=True, vmem_limit_bytes=VMEM_LIMIT
@@ -863,8 +880,8 @@
         solve,
         out_shape=[jax.ShapeDtypeStruct(block, F32)] * 4
         + [jax.ShapeDtypeStruct((1, WELLS), F32)],
-        in_specs=[vmem] * 21,
-        out_specs=[hbm] * 4 + [vmem],
+        in_specs=[vmem] * 22,
+        out_specs=[hbm] * 5,
         scratch_shapes=[
             pltpu.VMEM((4, 2, 16, C), F32),
             *[pltpu.VMEM(block, F32)] * 3,

time: 28.5 us -> 27.8 us (0.975)
  Pallas kernels: 27.7 us -> 27 us
    pallas_call x1, Pallas kernels: 2.18 us -> 1.65 us  [body(): pl.pallas_call(solve, out_shape=[jax.ShapeDtypeStruct(block, F32)] * 4 +...]
where the time goes in v4:
time: 27.8 us; the launch traced here: 27.6 us
  Pallas kernels  27 us (97%)
  between operations  0.64 us (2%)
    pallas_call x1, Pallas kernels, body(): pl.pallas_call(functools.partial(exchange, count_x, count_z), out_shape=[...  25.3 us
    pallas_call x1, Pallas kernels, body(): pl.pallas_call(solve, out_shape=[jax.ShapeDtypeStruct(block, F32)] * 4 +...  1.65 us

profile of v4, /device:TPU:24, one launch (start us, length us, event | category | flops | bytes accessed | tf_op | source)
XLA Modules:
  0.0 27.6 jit_solution(7219414505135673146)
XLA Ops:
  0.6 25.3 %exchange.1 = (f32[16,16,256]{2,1,0:T(8,128)S(1)}, f32[3,16,16,256]{3,2,1,0:T(8,128)S(1)}, f32[16,16,256]{2,1,0:T(8,128)S(1)}, f32[2,16,16,256]{3,2,1,0:T(8,128)...) custom-call(f32[16,16,256]{2,1,0:T(8,128)} %p_in.1, ...), custom_call_target="tpu_custom_call" | custom-call | tf_op jit(solution)/shard_map/exchange/pallas_call | solution.py:806
  26.0 1.7 %solve.1 = (f32[16,16,256]{2,1,0:T(8,128)}, f32[16,16,256]{2,1,0:T(8,128)}, f32[16,16,256]{2,1,0:T(8,128)}, f32[16,16,256]{2,1,0:T(8,128)}, f32[1,32]{1,0:T(1,128)}) custom-call(f32[16,16,256]{2,1,0:T(8,128)S(1)} %get-tuple-element.32.storage, f32[3,16,16,256]{3,2,1,0:T(8,128)S(1)} %get-tuple-element.33.local, f32[16,16,256]{2,1,0:T(8,128)S(1)} %get-tuple-element.34.frac, ...), custom_call_target="tpu_custom_call" | custom-call | tf_op jit(solution)/shard_map/solve/pallas_call | solution.py:879

commit v5 on v4

--- a/solution.py
+++ b/solution.py
@@ -221,7 +221,7 @@
 
         return carry
 
-    for s in (0, 1):
+    for s in (1, 0):
 
         @pl.when(has[s])
         def _():
@@ -402,7 +402,7 @@
             near.append((*ok, copy))
         bulk.append((*ok, remote(bulk_out.at[side], bulk_in.at[side], 15 + side, 10 + side, to)))
         mid.append((*ok, remote(mid_out.at[side], mid_in.at[side], side, 27 + side, to)))
-        last.append((*ok, remote(last_out.at[side], last_in.at[side], 19 + side, 14 + side, to)))
+        last.append((*ok, remote(last_out.at[side], last_in.at[side], 8 + side, 14 + side, to)))
     for side in (0, 1):
         ok, to = (has[side ^ 1], has[side]), target(side)
         perf.append((*ok, remote(perf_out.at[side], perf_in.at[side], 8 + side, 8 + side, to)))
@@ -628,6 +628,14 @@
         last_corner_out[c, 1:2] = num[m, k : k + 1, :]
         last_corner_out[c, 2:3] = second[m, k2 : k2 + 1, :]
         last_corner_out[c, 3:4] = second[m2, k : k + 1, :]
+    sent(perf)
+    for dx in (1, -1, 0):
+        out = True if dx == 0 else has[1 if dx > 0 else 0]
+
+        @pl.when(out)
+        def _():
+            group_wait(dx, send_sem.at[11 - dx])
+
     start(last)
 
     for l in range(L):
@@ -640,19 +648,21 @@
         frac_next[0, l] = shift_rows(part, -1)
         frac_next[1, l] = shift_columns(part, -1)
 
-    sent(perf)
-    for dx in (1, -1, 0):
-        out = True if dx == 0 else has[1 if dx > 0 else 0]
-
-        @pl.when(out)
-        def _():
-            group_wait(dx, send_sem.at[11 - dx])
-
     arrive(bulk)
     sent(bulk)
 
 
     arrive(mid)
+    for side in SIDES:
+        k = near_end(side)
+        behind = 14 if k else 1
+        change = weight[side] * planes(mid_in, side, 0)
+        add_to_plane(third, side, k, change)
+        along, col = planes(bulk_out, side ^ 1, 0), planes(bulk_out, side ^ 1, 1)
+        across = plane(face.at[1 if side < 2 else 0], side, min(k, 14))
+        value = inner_sum(jnp.zeros((16, C), F32), change, None, None, None, None, along, col)
+        add_to_plane(fourth, side, k, value * plane(inverse, side, k))
+        add_to_plane(fourth, side, behind, across * change * plane(inverse, side, behind))
     sent(mid)
 
     arrive(last)
@@ -720,15 +730,7 @@
         along, col = planes(bulk_in, side, 0), planes(bulk_in, side, 1)
         parts.append(inner_sum(add, value, None, None, None, None, along, col))
     for side in SIDES:
-        k = near_end(side)
-        behind = 14 if k else 1
-        change = weight[side] * planes(mid_in, side, 0)
-        add_to_plane(third, side, k, change)
-        along, col = planes(bulk_out, side ^ 1, 0), planes(bulk_out, side ^ 1, 1)
-        across = plane(face.at[1 if side < 2 else 0], side, min(k, 14))
-        value = inner_sum(border[side] * rings[side], change, None, None, None, None, along, col)
-        add_to_plane(fourth, side, k, value * plane(inverse, side, k))
-        add_to_plane(fourth, side, behind, across * change * plane(inverse, side, behind))
+        add_to_plane(fourth, side, near_end(side), weight[side] * rings[side])
 
     writes.append(pltpu.make_async_copy(fourth, new_p, sems.at[0, 3]))
     writes[1].start()
@@ -852,7 +854,7 @@
             pltpu.VMEM((NP, WELLS), F32),
             pltpu.VMEM((1, WELLS), jnp.int32),
             pltpu.VMEM((1, WELLS), F32),
-            dma((23,)),
+            dma((19,)),
             dma((31,)),
         ],
         compiler_params=pltpu.CompilerParams(

time: 27.8 us -> 27.7 us (level)
  no operation moved by 1% of the time
where the time goes in v5:
time: 27.7 us; the launch traced here: 27.5 us
  Pallas kernels  26.9 us (97%)
  between operations  0.64 us (2%)
    pallas_call x1, Pallas kernels, body(): pl.pallas_call(functools.partial(exchange, count_x, count_z), out_shape=[...  25.2 us
    pallas_call x1, Pallas kernels, body(): pl.pallas_call(solve, out_shape=[jax.ShapeDtypeStruct(block, F32)] * 4 +...  1.62 us

profile of v5, /device:TPU:24, one launch (start us, length us, event | category | flops | bytes accessed | tf_op | source)
XLA Modules:
  0.0 27.5 jit_solution(14977212314627244665)
XLA Ops:
  0.6 25.2 %exchange.1 = (f32[16,16,256]{2,1,0:T(8,128)S(1)}, f32[3,16,16,256]{3,2,1,0:T(8,128)S(1)}, f32[16,16,256]{2,1,0:T(8,128)S(1)}, f32[2,16,16,256]{3,2,1,0:T(8,128)...) custom-call(f32[16,16,256]{2,1,0:T(8,128)} %p_in.1, ...), custom_call_target="tpu_custom_call" | custom-call | tf_op jit(solution)/shard_map/exchange/pallas_call | solution.py:808
  25.9 1.6 %solve.1 = (f32[16,16,256]{2,1,0:T(8,128)}, f32[16,16,256]{2,1,0:T(8,128)}, f32[16,16,256]{2,1,0:T(8,128)}, f32[16,16,256]{2,1,0:T(8,128)}, f32[1,32]{1,0:T(1,128)}) custom-call(f32[16,16,256]{2,1,0:T(8,128)S(1)} %get-tuple-element.32.storage, f32[3,16,16,256]{3,2,1,0:T(8,128)S(1)} %get-tuple-element.33.local, f32[16,16,256]{2,1,0:T(8,128)S(1)} %get-tuple-element.34.frac, ...), custom_call_target="tpu_custom_call" | custom-call | tf_op jit(solution)/shard_map/solve/pallas_call | solution.py:881

commit v6 on v5

--- a/solution.py
+++ b/solution.py
@@ -774,12 +774,13 @@
         saturation = source[l] - local[2, l] * out
         out_s[l] = saturation
         out_h[l] = jnp.maximum(local[1, l], saturation)
-        if l % 8 == 7:
-            part = pl.ds(l - 7, 8)
+        if l in (7, 12, 15):
+            chunk = (7, 12, 15).index(l)
+            part = (pl.ds(0, 8), pl.ds(8, 5), pl.ds(13, 3))[chunk]
             for n, (src, dst) in enumerate(
                 ((out_r, residual), (out_s, new_s), (out_h, new_h))
             ):
-                copy = pltpu.make_async_copy(src.at[part], dst.at[part], sems.at[l // 8, n])
+                copy = pltpu.make_async_copy(src.at[part], dst.at[part], sems.at[chunk, n])
                 copy.start()
                 writes.append(copy)
     for copy in writes:
@@ -887,7 +888,7 @@
         scratch_shapes=[
             pltpu.VMEM((4, 2, 16, C), F32),
             *[pltpu.VMEM(block, F32)] * 3,
-            dma((2, 4)),
+            dma((3, 4)),
         ],
         compiler_params=pltpu.CompilerParams(vmem_limit_bytes=VMEM_LIMIT),
         name="solve",

time: 27.7 us -> 27.7 us (level)
  no operation moved by 1% of the time
where the time goes in v6:
time: 27.7 us; the launch traced here: 27.5 us
  Pallas kernels  26.9 us (97%)
  between operations  0.64 us (2%)
    pallas_call x1, Pallas kernels, body(): pl.pallas_call(functools.partial(exchange, count_x, count_z), out_shape=[...  25.2 us
    pallas_call x1, Pallas kernels, body(): pl.pallas_call(solve, out_shape=[jax.ShapeDtypeStruct(block, F32)] * 4 +...  1.62 us

profile of v6, /device:TPU:24, one launch (start us, length us, event | category | flops | bytes accessed | tf_op | source)
XLA Modules:
  0.0 27.5 jit_solution(10442634221575509917)
XLA Ops:
  0.6 25.2 %exchange.1 = (f32[16,16,256]{2,1,0:T(8,128)S(1)}, f32[3,16,16,256]{3,2,1,0:T(8,128)S(1)}, f32[16,16,256]{2,1,0:T(8,128)S(1)}, f32[2,16,16,256]{3,2,1,0:T(8,128)...) custom-call(f32[16,16,256]{2,1,0:T(8,128)} %p_in.1, ...), custom_call_target="tpu_custom_call" | custom-call | tf_op jit(solution)/shard_map/exchange/pallas_call | solution.py:809
  25.9 1.6 %solve.1 = (f32[16,16,256]{2,1,0:T(8,128)}, f32[16,16,256]{2,1,0:T(8,128)}, f32[16,16,256]{2,1,0:T(8,128)}, f32[16,16,256]{2,1,0:T(8,128)}, f32[1,32]{1,0:T(1,128)}) custom-call(f32[16,16,256]{2,1,0:T(8,128)S(1)} %get-tuple-element.32.storage, f32[3,16,16,256]{3,2,1,0:T(8,128)S(1)} %get-tuple-element.33.local, f32[16,16,256]{2,1,0:T(8,128)S(1)} %get-tuple-element.34.frac, ...), custom_call_target="tpu_custom_call" | custom-call | tf_op jit(solution)/shard_map/solve/pallas_call | solution.py:882
